TPU v7x, 32 devices: a whole 2x2x4 slice. The times are simulated.
32 devices in a mesh: row: 8 (over z, x), col: 4 (over y, core).
Axes of the slice: x: 2, y: 2, z: 4, core: 2. Of those that a mesh axis runs over, the one named last changes fastest.
Arguments:
- feat: bfloat16 [256, 128, 256], P('row', 'col'), may hold values from -6 to 6
- noise_fine: float32 [256, 128, 256], P('row', 'col'), may hold values from -0.5 to 0.5
- noise_coarse: float32 [128, 64, 256], P('row', 'col'), may hold values from -0.5 to 0.5
- w_post: bfloat16 [2304, 256], replicated, may hold values from -0.125 to 0.125
- w_coarse: bfloat16 [2304, 256], replicated, may hold values from -0.125 to 0.125
- w_prior: bfloat16 [2304, 512], replicated, may hold values from -0.125 to 0.125
Outputs:
- grad_feat: bfloat16 [256, 128, 256], P('row', 'col')
- grad_post: float32 [589824], P(('row', 'col'))
- grad_coarse: float32 [589824], P(('row', 'col'))
- grad_prior: float32 [1179648], P(('row', 'col'))
All inputs are finite; a program needn't handle non-finite values.
Results may differ from a plain program's by a relative error of at most 0.0075.
Values may be sent and summed in bfloat16 or wider, within the bound.
A program may use at most 128 MiB of HBM per device.

v0:
```python
import functools
import math

import jax
import jax.numpy as jnp
from jax import lax
from jax.experimental import pallas as pl
from jax.experimental.pallas import tpu as pltpu
from jax.sharding import PartitionSpec as P

F32 = jnp.float32
BF16 = jnp.bfloat16
EDGE = 8


LANES = 128


def put(ref, at, values):
    for d in range(ref.shape[0]):
        ref[d, at, :] = values[:, d * LANES : (d + 1) * LANES]


def get(ref, at):
    return jnp.concatenate([ref[d, at, :] for d in range(ref.shape[0])], axis=1)


def tile_kernel(
    dims,
    feat,
    noise_fine,
    noise_coarse,
    w_post,
    w_coarse,
    w_prior,
    grad_feat,
    out_post,
    out_coarse,
    out_prior,
    fine,
    err,
    coarse,
    mix,
    s_feat,
    s_pool,
    s_dpr,
    x_feat,
    x_pool,
    x_ctx,
    x_dpr,
    x_gco,
    x_gfi,
    edge_fine,
    edge_coarse,
    edge_dpr,
    sums,
    outgoing,
    incoming,
    sems,
    chain_sems,
):
    s_ctx = s_gfi = s_feat
    s_gco = s_pool
    rows, cols, chans, scale, n_row, n_col = dims
    half_rows, half_cols = rows // 2, cols // 2
    r = lax.axis_index("row")
    c = lax.axis_index("col")
    has_up, has_down = r > 0, r < n_row - 1
    has_left, has_right = c > 0, c < n_col - 1
    sides = (
        (has_up, {"row": r - 1}),
        (has_down, {"row": r + 1}),
        (has_left, {"col": c - 1}),
        (has_right, {"col": c + 1}),
    )
    edge_fine[...] = jnp.zeros_like(edge_fine)
    edge_coarse[...] = jnp.zeros_like(edge_coarse)
    edge_dpr[...] = jnp.zeros_like(edge_dpr)
    for x, width, height in (
        (x_feat, cols, rows),
        (x_pool, half_cols, half_rows),
        (x_ctx, cols, rows),
        (x_dpr, cols, rows),
        (x_gco, half_cols, half_rows),
        (x_gfi, cols, rows),
    ):
        x[0:width, :] = jnp.zeros((width, x.shape[1]), x.dtype)
        x[(height + 1) * width :, :] = jnp.zeros((width, x.shape[1]), x.dtype)

    barrier = pltpu.get_barrier_semaphore()
    for has, device in sides:
        @pl.when(has)
        def _(device=device):
            pl.semaphore_signal(
                barrier, inc=1, device_id=device, device_id_type=pl.DeviceIdType.MESH
            )
    count = n_row * n_col
    bits = count.bit_length() - 1
    col_bits = n_col.bit_length() - 1
    me = r * n_col + c

    def bit_of(b):
        return me // 2**b % 2

    def partner(b):
        if b < col_bits:
            return {"col": c + 2**b * (1 - 2 * bit_of(b))}
        return {"row": r + 2 ** (b - col_bits) * (1 - 2 * bit_of(b))}

    for b in range(bits):
        pl.semaphore_signal(
            barrier, inc=1, device_id=partner(b), device_id_type=pl.DeviceIdType.MESH
        )
    pl.semaphore_wait(barrier, bits + sum(has.astype(jnp.int32) for has, _device in sides))

    def each(n, body):
        if n <= 16:
            for j in range(n):
                body(j)
        else:
            pl.loop(0, n)(body)

    def chain(number, order, out, out_at):
        acc, send, recv = sums[number], outgoing[number], incoming[number]
        state = {"step": 0, "copy": None}

        def offset(k):
            return count - (count >> k)

        def step():
            k = state["step"]
            if k > bits:
                return
            state["step"] = k + 1
            if k > 0:
                state["copy"].wait()
            if k == bits:
                total = acc[me] + recv[offset(k - 1)].astype(F32)
                per = total.shape[0]
                stride = out.shape[0] // per
                for d in range(total.shape[1] // LANES):
                    out[pl.ds(out_at // LANES + d, per, stride=stride), :] = total[
                        :, d * LANES : (d + 1) * LANES
                    ]
                return
            bit = order[k]
            free = [b for b in range(bits) if b not in order[:k]]
            rest = [b for b in free if b != bit]
            place = free.index(bit)
            fixed = sum((bit_of(b) * 2**b for b in order[:k]), 0)
            n = count >> (k + 1)

            def value(j, choice):
                index = fixed + choice * 2**bit
                for q, b in enumerate(rest):
                    index = index + j // 2**q % 2 * 2**b
                total = acc[index]
                if k > 0:
                    slot = j // 2**place * 2 ** (place + 1) + choice * 2**place + j % 2**place
                    total = total + recv[offset(k - 1) + slot].astype(F32)
                return index, total

            def fill(j):
                send[offset(k) + j] = value(j, 1 - bit_of(bit))[1].astype(BF16)

            each(n, fill)
            state["copy"] = pltpu.make_async_remote_copy(
                src_ref=send.at[pl.ds(offset(k), n)],
                dst_ref=recv.at[pl.ds(offset(k), n)],
                send_sem=chain_sems.at[number, k, 0],
                recv_sem=chain_sems.at[number, k, 1],
                device_id=partner(bit),
                device_id_type=pl.DeviceIdType.MESH,
            )
            state["copy"].start()

            def keep(j):
                index, total = value(j, bit_of(bit))
                acc[index] = total

            if k > 0:
                each(n, keep)

        return step

    near, rest = [0], list(range(1, bits))
    first = near + rest
    second = near + rest[1::-1] + rest[2:]
    third = near + rest[2:3] + rest[:2] + rest[3:]
    half = chans // 2
    post_1 = chain(0, first, out_post, 0)
    post_2 = chain(1, second, out_post, half)
    middle = chain(2, third, out_coarse, 0)
    prior_1 = chain(3, first, out_prior, 0)
    prior_2 = chain(4, second, out_prior, chans)
    parts_post = ((sums[0], 0), (sums[1], half))
    parts_coarse = ((sums[2], 0),)
    parts_prior = ((sums[3], 0), (sums[4], chans))

    def spread(parts, start, values):
        height = values.shape[0]
        for acc, at in parts:
            per, width = acc.shape[1:]
            row = start
            while row < start + height:
                inner = row % per
                size = min(per - inner, start + height - row)
                acc[row // per, inner : inner + size] = values[
                    row - start : row - start + size, at : at + width
                ]
                row += size

    def exchange(index, s, x, edges, slot, height, width, work_1=None, work_2=None):
        stride = width + 2 * EDGE
        depth = s.shape[0] * LANES

        def copy(src, dst, k, device):
            return pltpu.make_async_remote_copy(
                src_ref=src,
                dst_ref=dst,
                send_sem=sems.at[index, k],
                recv_sem=sems.at[index, 4 + k],
                device_id=device,
                device_id_type=pl.DeviceIdType.MESH,
            )

        edges[slot, 0] = get(s, pl.ds(EDGE, height, stride=stride)).astype(BF16)
        edges[slot, 1] = get(s, pl.ds(EDGE + width - 1, height, stride=stride)).astype(BF16)
        leftward = copy(edges.at[slot, 0], edges.at[slot, 3], 0, {"col": c - 1})
        rightward = copy(edges.at[slot, 1], edges.at[slot, 2], 1, {"col": c + 1})
        pl.when(has_left)(leftward.start)
        pl.when(has_right)(rightward.start)
        for i in range(height):
            x[pl.ds((i + 1) * width, width), depth : 2 * depth] = get(
                s, pl.ds(i * stride + EDGE, width)
            ).astype(BF16)
        if work_1 is not None:
            work_1()

        @pl.when(has_left)
        def _():
            leftward.wait_send()
            rightward.wait_recv()

        @pl.when(has_right)
        def _():
            rightward.wait_send()
            leftward.wait_recv()

        put(s, pl.ds(EDGE - 1, height, stride=stride), edges[slot, 2].astype(F32))
        put(s, pl.ds(EDGE + width, height, stride=stride), edges[slot, 3].astype(F32))
        order = [0, height - 1] + list(range(1, height - 1))
        upward = copy(
            x.at[pl.ds(width, width)], x.at[pl.ds((height + 1) * width, width)], 2, {"row": r - 1}
        )
        downward = copy(
            x.at[pl.ds(height * width, width)], x.at[pl.ds(0, width)], 3, {"row": r + 1}
        )
        for n, i in enumerate(order):
            for b in (0, 2):
                x[pl.ds((i + 1) * width, width), b * depth : (b + 1) * depth] = get(
                    s, pl.ds(i * stride + EDGE - 1 + b, width)
                ).astype(BF16)
            if n == 1:
                pl.when(has_up)(upward.start)
                pl.when(has_down)(downward.start)
        if work_2 is not None:
            work_2()

        @pl.when(has_up)
        def _():
            upward.wait_send()
            downward.wait_recv()

        @pl.when(has_down)
        def _():
            downward.wait_send()
            upward.wait_recv()

    def conv(x, w, start, size, width):
        k = w.shape[0] // 3
        total = None
        for a in range(3):
            part = jnp.dot(
                x[pl.ds(start + a * width, size), :],
                w[a * k : (a + 1) * k, :],
                preferred_element_type=F32,
            )
            total = part if total is None else total + part
        return total

    def conv_back(x, w, start, size, width):
        k = w.shape[0] // 9
        depth = w.shape[1]
        total = None
        for a in range(3):
            for b in range(3):
                tap = 3 * (2 - a) + (2 - b)
                part = lax.dot_general(
                    x[pl.ds(start + a * width, size), b * depth : (b + 1) * depth],
                    w[tap * k : (tap + 1) * k, :],
                    (((1,), (1,)), ((), ())),
                    preferred_element_type=F32,
                )
                total = part if total is None else total + part
        return total

    def weight_grad(x, g, parts, height, width, taps):
        depth = x.shape[1] // 3
        g_depth = g.shape[1] // 3
        size = height * width
        own = g[pl.ds(width, size), g_depth : 2 * g_depth]
        for a in taps:
            for b in range(3):
                tap = 3 * a + b
                values = scale * lax.dot_general(
                    x[pl.ds(a * width, size), b * depth : (b + 1) * depth],
                    own,
                    (((0,), (0,)), ((), ())),
                    preferred_element_type=F32,
                )
                spread(parts, tap * depth, values)

    lines = 8
    block = lines * cols
    half_block = block // 4

    def pool_sum(values):
        paired = values.reshape(lines // 2, 2, cols, chans)
        put(mix, pl.ds(0, block // 2), (paired[:, 0] + paired[:, 1]).reshape(block // 2, chans))
        return get(mix, pl.ds(0, half_block, stride=2)) + get(mix, pl.ds(1, half_block, stride=2))

    def repeat_columns(values):
        put(mix, pl.ds(0, half_rows * half_cols, stride=2), values)
        put(mix, pl.ds(1, half_rows * half_cols, stride=2), values)

    fine_stride = cols + 2 * EDGE
    half_stride = half_cols + 2 * EDGE

    for i in range(rows):
        put(s_feat, pl.ds(i * fine_stride + EDGE, cols), feat[pl.ds(i * cols, cols), :].astype(F32))
    exchange(0, s_feat, x_feat, edge_fine, 0, rows, cols)

    for m in range(rows // lines):
        values = conv(x_feat, w_post, m * block, block, cols) + noise_fine[pl.ds(m * block, block), :]
        fine[pl.ds(m * block, block), :] = values
        pooled = (0.25 * pool_sum(values)).astype(BF16).astype(F32)
        for i in range(lines // 2):
            at = pl.ds((m * lines // 2 + i) * half_stride + EDGE, half_cols)
            put(s_pool, at, pooled[i * half_cols : (i + 1) * half_cols])
    exchange(1, s_pool, x_pool, edge_coarse, 0, half_rows, half_cols)

    values = conv(x_pool, w_coarse, 0, half_rows * half_cols, half_cols) + noise_coarse[...]
    coarse[...] = values
    repeat_columns(values.astype(BF16).astype(F32))
    for i in range(rows):
        put(s_ctx, pl.ds(i * fine_stride + EDGE, cols), get(mix, pl.ds(i // 2 * cols, cols)))
    exchange(2, s_ctx, x_ctx, edge_fine, 1, rows, cols)

    for m in range(rows // lines):
        prior = conv(x_ctx, w_prior, m * block, block, cols)
        raw = prior[:, chans:]
        small = jnp.exp(-jnp.abs(raw))
        sigma = jnp.maximum(raw, 0.0) + jnp.log1p(small) + 0.5
        gate = jnp.where(raw >= 0, 1.0, small) / (1.0 + small)
        inverse = 1.0 / sigma
        deviation = fine[pl.ds(m * block, block), :] - prior[:, :chans]
        ratio = deviation * inverse
        residual = ratio * inverse
        err[pl.ds(m * block, block), :] = residual
        slope = (inverse - ratio * ratio * inverse) * gate
        for i in range(lines):
            at = pl.ds((m * lines + i) * fine_stride + EDGE, cols)
            here = slice(i * cols, (i + 1) * cols)
            both = jnp.concatenate([-residual[here], slope[here]], axis=1)
            put(s_dpr, at, both.astype(BF16).astype(F32))
    exchange(
        3,
        s_dpr,
        x_dpr,
        edge_dpr,
        0,
        rows,
        cols,
        lambda: weight_grad(x_ctx, x_dpr, parts_prior, rows, cols, (0, 1)),
        lambda: weight_grad(x_ctx, x_dpr, parts_prior, rows, cols, (2,)),
    )

    prior_1()
    prior_2()
    for m in range(rows // lines):
        if m == 2:
            prior_1()
            prior_2()
        back = pool_sum(conv_back(x_dpr, w_prior, m * block, block, cols))
        g = (coarse[pl.ds(m * half_block, half_block), :] + back).astype(BF16).astype(F32)
        for i in range(lines // 2):
            at = pl.ds((m * lines // 2 + i) * half_stride + EDGE, half_cols)
            put(s_gco, at, g[i * half_cols : (i + 1) * half_cols])
    exchange(
        4,
        s_gco,
        x_gco,
        edge_coarse,
        1,
        half_rows,
        half_cols,
        lambda: weight_grad(x_pool, x_gco, parts_coarse, half_rows, half_cols, (0, 1)),
        lambda: weight_grad(x_pool, x_gco, parts_coarse, half_rows, half_cols, (2,)),
    )

    prior_1()
    prior_2()
    middle()
    repeat_columns(0.25 * conv_back(x_gco, w_coarse, 0, half_rows * half_cols, half_cols))
    for i in range(rows):
        total = err[pl.ds(i * cols, cols), :] + get(mix, pl.ds(i // 2 * cols, cols))
        put(s_gfi, pl.ds(i * fine_stride + EDGE, cols), total.astype(BF16).astype(F32))
    def late_work():
        prior_1()
        prior_2()
        middle()
        weight_grad(x_feat, x_gfi, parts_post, rows, cols, (2,))

    exchange(
        5,
        s_gfi,
        x_gfi,
        edge_fine,
        2,
        rows,
        cols,
        lambda: weight_grad(x_feat, x_gfi, parts_post, rows, cols, (0, 1)),
        late_work,
    )
    post_1()
    post_2()
    for m in range(rows // lines):
        if m == 2:
            post_1()
            post_2()
            prior_1()
            prior_2()
        grad_feat[pl.ds(m * block, block), :] = conv_back(
            x_gfi, w_post, m * block, block, cols
        ).astype(BF16)
    for _ in range(bits + 1):
        for step in (prior_1, prior_2, middle, post_1, post_2):
            step()


def hand_out(*refs):
    for source, target in zip(refs[:4], refs[4:]):
        target[...] = source[...]


def on_device(sizes, feat, noise_fine, noise_coarse, w_post, w_coarse, w_prior):
    n_row, n_col = sizes
    rows, cols, chans = feat.shape
    half_rows, half_cols = rows // 2, cols // 2
    scale = 1.0 / math.sqrt(rows * n_row * cols * n_col)
    cells, half_cells = rows * cols, half_rows * half_cols
    vmem = pl.BlockSpec(memory_space=pltpu.VMEM)

    def padded(height, width, depth):
        return pltpu.VMEM((depth // LANES, height * (width + 2 * EDGE), LANES), F32)

    def columns(height, width, depth):
        return pltpu.VMEM(((height + 2) * width, 3 * depth), BF16)

    dims = (rows, cols, chans, scale, n_row, n_col)
    count = n_row * n_col
    per = w_post.shape[0] // count
    widths = (chans // 2, chans // 2, chans, chans, chans)
    grad_feat, out_post, out_coarse, out_prior = pl.pallas_call(
        functools.partial(tile_kernel, dims),
        out_shape=(
            jax.ShapeDtypeStruct((cells, chans), BF16),
            jax.ShapeDtypeStruct((per * chans // LANES, LANES), F32),
            jax.ShapeDtypeStruct((per * chans // LANES, LANES), F32),
            jax.ShapeDtypeStruct((per * 2 * chans // LANES, LANES), F32),
        ),
        in_specs=[vmem] * 6,
        out_specs=(vmem,) * 4,
        scratch_shapes=[
            pltpu.VMEM((cells, chans), F32),
            pltpu.VMEM((cells, chans), F32),
            pltpu.VMEM((half_cells, chans), F32),
            pltpu.VMEM((chans // LANES, 2 * half_cells, LANES), F32),
            padded(rows, cols, chans),
            padded(half_rows, half_cols, chans),
            padded(rows, cols, 2 * chans),
            columns(rows, cols, chans),
            columns(half_rows, half_cols, chans),
            columns(rows, cols, chans),
            columns(rows, cols, 2 * chans),
            columns(half_rows, half_cols, chans),
            columns(rows, cols, chans),
            pltpu.VMEM((3, 4, rows, chans), BF16),
            pltpu.VMEM((2, 4, half_rows, chans), BF16),
            pltpu.VMEM((1, 4, rows, 2 * chans), BF16),
            [pltpu.VMEM((count, per, width), F32) for width in widths],
            [pltpu.VMEM((count - 1, per, width), BF16) for width in widths],
            [pltpu.VMEM((count - 1, per, width), BF16) for width in widths],
            pltpu.SemaphoreType.DMA((6, 8)),
            pltpu.SemaphoreType.DMA((5, count.bit_length() - 1, 2)),
        ],
        compiler_params=pltpu.CompilerParams(
            collective_id=0, has_side_effects=True, vmem_limit_bytes=65000 * 1024
        ),
    )(
        feat.reshape(cells, chans),
        noise_fine.reshape(cells, chans),
        noise_coarse.reshape(half_cells, chans),
        w_post,
        w_coarse,
        w_prior,
    )
    results = (grad_feat, out_post, out_coarse, out_prior)
    grad_feat, out_post, out_coarse, out_prior = pl.pallas_call(
        hand_out,
        out_shape=tuple(jax.ShapeDtypeStruct(a.shape, a.dtype) for a in results),
        in_specs=[vmem] * 4,
        out_specs=(vmem,) * 4,
    )(*results)
    return (
        grad_feat.reshape(rows, cols, chans),
        out_post.reshape(-1),
        out_coarse.reshape(-1),
        out_prior.reshape(-1),
    )


def solution(mesh):
    sizes = (mesh.shape["row"], mesh.shape["col"])
    return jax.shard_map(
        functools.partial(on_device, sizes),
        mesh=mesh,
        in_specs=(
            P("row", "col", None),
            P("row", "col", None),
            P("row", "col", None),
            P(),
            P(),
            P(),
        ),
        out_specs=(P("row", "col", None), P(("row", "col")), P(("row", "col")), P(("row", "col"))),
        check_vma=False,
    )
```

profile of v0, /device:TPU:0, one launch (start us, length us, event | category | flops | bytes accessed | tf_op | source)
XLA Modules:
  0.0 84.4 jit_solution(15514837185758705088)
XLA Ops:
  0.6 81.7 %shard_map.93 = (bf16[1024,256]{1,0:T(8,128)(2,1)}, f32[144,128]{1,0:T(8,128)}, f32[144,128]{1,0:T(8,128)}, f32[288,128]{1,0:T(8,128)}) custom-call(bf16[1024,256]{1,0:T(8,128)(2,1)} %bitcast.8, f32[1024,256]{1,0:T(8,128)} %bitcast.7, f32[256,256]{1,0:T(8,128)} %bitcast.9, bf16[2304,256]{1,0:T(8,128)(2,1)} %w_post.1, bf16[2304,256]{1,0:T(8,128)(2,1)} %w_coarse.1, ...), custom_call_target="tpu_custom_call" | custom-call | tf_op jit(solution)/shard_map/pallas_call | solution.py:475
  82.4 2.0 %shard_map.94 = (bf16[1024,256]{1,0:T(8,128)(2,1)}, f32[144,128]{1,0:T(8,128)}, f32[144,128]{1,0:T(8,128)}, f32[288,128]{1,0:T(8,128)}) custom-call(bf16[1024,256]{1,0:T(8,128)(2,1)} %get-tuple-element.12.refs_0_, f32[144,128]{1,0:T(8,128)} %get-tuple-element.13.refs_1_, f32[144,128]{1,0:T(8,128)} %get-tuple-element.14.refs_2_, ...), custom_call_target="tpu_custom_call" | custom-call | tf_op jit(solution)/shard_map/pallas_call | solution.py:520
where the time goes:
time: 84.5 us; the launch traced here: 84.4 us
  Pallas kernels  83.8 us (99%)
    pallas_call x1, Pallas kernels, on_device(): pl.pallas_call(functools.partial(tile_kernel, dims), out_shape=(jax.Shape...  81.7 us
    pallas_call x1, Pallas kernels, on_device(): pl.pallas_call(hand_out, out_shape=tuple((jax.ShapeDtypeStruct(a.shape, a...  2.03 us

commit v1 on v0

v1 whole, which is shorter than its diff:
```python
import functools
import math

import jax
import jax.numpy as jnp
from jax import lax
from jax.experimental import pallas as pl
from jax.experimental.pallas import tpu as pltpu
from jax.sharding import PartitionSpec as P

F32 = jnp.float32
BF16 = jnp.bfloat16
EDGE = 8


LANES = 128


def put(ref, at, values):
    for d in range(values.shape[1] // LANES):
        ref[d, at, :] = values[:, d * LANES : (d + 1) * LANES]


def get(ref, at):
    return jnp.concatenate([ref[d, at, :] for d in range(ref.shape[0])], axis=1)


DIRECTIONS = ((-1, 0), (1, 0), (0, -1), (0, 1), (-1, -1), (-1, 1), (1, -1), (1, 1))
OPPOSITE = (1, 0, 3, 2, 7, 6, 5, 4)
UP, DOWN, LEFT, RIGHT, UP_LEFT, UP_RIGHT, DOWN_LEFT, DOWN_RIGHT = range(8)
TAPS = (((0,), (1, 2)), ((0, 1), (2,)))


def round_up(n, m):
    return -(-n // m) * m


def tile_kernel(
    dims,
    feat,
    noise_fine,
    noise_coarse,
    w_post,
    w_coarse,
    w_prior,
    grad_feat,
    out_post,
    out_coarse,
    out_prior,
    fine,
    err,
    coarse,
    s_fine,
    s_pool,
    s_noise,
    s_ctx,
    s_pair,
    x_feat,
    x_pool,
    side_pool,
    x_ctx,
    side_ctx,
    w_sums,
    g_main,
    g_side,
    boxes,
    own_gfi,
    edges,
    halos,
    sums,
    outgoing,
    incoming,
    sems,
    chain_sems,
):
    x_gco, x_gfi = x_ctx, x_feat
    rows, cols, chans, scale, n_row, n_col = dims
    mix = s_pair.at[0, pl.ds(0, chans // LANES)]
    h, w = rows // 2, cols // 2
    cells = h * w
    r = lax.axis_index("row")
    c = lax.axis_index("col")
    has_up, has_down = r > 0, r < n_row - 1
    has_left, has_right = c > 0, c < n_col - 1
    vertical = {-1: has_up, 0: None, 1: has_down}
    horizontal = {-1: has_left, 0: None, 1: has_right}

    def neighbour(d):
        down, right = DIRECTIONS[d]
        device = {}
        if down:
            device["row"] = r + down
        if right:
            device["col"] = c + right
        if not right:
            return vertical[down], device
        if not down:
            return horizontal[right], device
        return jnp.logical_and(vertical[down], horizontal[right]), device

    sides = [neighbour(d) for d in range(8)]

    halos[...] = jnp.zeros_like(halos)
    barrier = pltpu.get_barrier_semaphore()
    for has, device in sides:
        @pl.when(has)
        def _(device=device):
            pl.semaphore_signal(
                barrier, inc=1, device_id=device, device_id_type=pl.DeviceIdType.MESH
            )
    count = n_row * n_col
    bits = count.bit_length() - 1
    col_bits = n_col.bit_length() - 1
    me = r * n_col + c

    def bit_of(b):
        return me // 2**b % 2

    def partner(b):
        if b < col_bits:
            return {"col": c + 2**b * (1 - 2 * bit_of(b))}
        return {"row": r + 2 ** (b - col_bits) * (1 - 2 * bit_of(b))}

    for b in range(bits):
        pl.semaphore_signal(
            barrier, inc=1, device_id=partner(b), device_id_type=pl.DeviceIdType.MESH
        )

    for ref in (s_fine, s_pool, s_noise, s_ctx, fine):
        ref[...] = jnp.zeros_like(ref)

    def enter():
        pl.semaphore_wait(barrier, bits + sum(has.astype(jnp.int32) for has, _device in sides))

    def each(n, body):
        if n <= 16:
            for j in range(n):
                body(j)
        else:
            pl.loop(0, n)(body)

    def chain(number, order, out, out_at):
        acc, send, recv = sums[number], outgoing[number], incoming[number]
        state = {"step": 0, "copy": None}

        def offset(k):
            return count - (count >> k)

        def step():
            k = state["step"]
            if k > bits:
                return
            state["step"] = k + 1
            if k > 0:
                state["copy"].wait()
            if k == bits:
                total = acc[me] + recv[offset(k - 1)].astype(F32)
                per = total.shape[0]
                stride = out.shape[0] // per
                for d in range(total.shape[1] // LANES):
                    out[pl.ds(out_at // LANES + d, per, stride=stride), :] = total[
                        :, d * LANES : (d + 1) * LANES
                    ]
                return
            bit = order[k]
            free = [b for b in range(bits) if b not in order[:k]]
            rest = [b for b in free if b != bit]
            place = free.index(bit)
            fixed = sum((bit_of(b) * 2**b for b in order[:k]), 0)
            n = count >> (k + 1)

            def value(j, choice):
                index = fixed + choice * 2**bit
                for q, b in enumerate(rest):
                    index = index + j // 2**q % 2 * 2**b
                total = acc[index]
                if k > 0:
                    slot = j // 2**place * 2 ** (place + 1) + choice * 2**place + j % 2**place
                    total = total + recv[offset(k - 1) + slot].astype(F32)
                return index, total

            def fill(j):
                send[j] = value(j, 1 - bit_of(bit))[1].astype(BF16)

            each(n, fill)
            state["copy"] = pltpu.make_async_remote_copy(
                src_ref=send.at[pl.ds(0, n)],
                dst_ref=recv.at[pl.ds(offset(k), n)],
                send_sem=chain_sems.at[number, k, 0],
                recv_sem=chain_sems.at[number, k, 1],
                device_id=partner(bit),
                device_id_type=pl.DeviceIdType.MESH,
            )
            state["copy"].start()

            def keep(j):
                index, total = value(j, bit_of(bit))
                acc[index] = total

            if k > 0:
                each(n, keep)

        return step


    near, rest = [0], list(range(1, bits))
    first = near + rest
    second = near + rest[1::-1] + rest[2:]
    third = near + rest[2:3] + rest[:2] + rest[3:]
    half = chans // 2
    post_1 = chain(0, first, out_post, 0)
    post_2 = chain(1, second, out_post, half)
    middle = chain(2, third, out_coarse, 0)
    prior_1 = chain(3, first, out_prior, 0)
    prior_2 = chain(4, second, out_prior, chans)
    parts_post = ((sums[0], 0), (sums[1], half))
    parts_coarse = ((sums[2], 0),)
    parts_prior = ((sums[3], 0), (sums[4], chans))

    def spread(parts, start, values):
        height = values.shape[0]
        for acc, at in parts:
            per, width = acc.shape[1:]
            row = start
            while row < start + height:
                inner = row % per
                size = min(per - inner, start + height - row)
                acc[row // per, inner : inner + size] = values[
                    row - start : row - start + size, at : at + width
                ]
                row += size


    def copies(index, sizes):
        found = []
        for d in range(8):
            size = sizes[0] if d < 4 else sizes[1]
            found.append(
                pltpu.make_async_remote_copy(
                    src_ref=edges.at[index, d, pl.ds(0, size)],
                    dst_ref=halos.at[index, OPPOSITE[d], pl.ds(0, size)],
                    send_sem=sems.at[index, d],
                    recv_sem=sems.at[index, 8 + OPPOSITE[d]],
                    device_id=sides[d][1],
                    device_id_type=pl.DeviceIdType.MESH,
                )
            )
        return found

    def start(index, sizes, parts):
        found = copies(index, sizes)
        for d in (4, 5, 6, 7, 0, 1, 2, 3):
            at = 0
            for part in parts[d]:
                edges[index, d, at : at + part.shape[0], :] = part.astype(BF16)
                at += part.shape[0]
            pl.when(sides[d][0])(found[d].start)
        return found

    def finish(found):
        for d in range(8):
            @pl.when(sides[d][0])
            def _(d=d):
                found[d].wait_send()
                found[OPPOSITE[d]].wait_recv()

    def halo(index, d, at, size):
        return halos[index, d, at : at + size, :].astype(F32)

    def view(x, t, u):
        return x[t % 2, u + 1, pl.ds(w if t >= 1 else 0, cells), :]

    def dot_in(x, g):
        return lax.dot_general(x, g, (((0,), (0,)), ((), ())), preferred_element_type=F32)

    def dot_out(g, weights):
        return lax.dot_general(g, weights, (((1,), (1,)), ((), ())), preferred_element_type=F32)

    def tap_of(weights, a, b):
        k = weights.shape[0] // 9
        return weights[(3 * a + b) * k : (3 * a + b + 1) * k, :]

    fine_stride = cols + 2 * EDGE
    stride = w + 2 * EDGE
    extra = round_up(h + 1, 16)
    side = round_up(h + 2, 8)
    phases = [(p, q) for p in range(2) for q in range(2)]

    for i in range(rows):
        put(
            s_fine,
            pl.ds((i + 1) * fine_stride + EDGE, cols),
            feat[pl.ds(i * cols, cols), :].astype(F32),
        )
    for i in range(h):
        put(s_noise, pl.ds((i + 1) * stride + EDGE, w), noise_coarse[pl.ds(i * w, w), :])
    top, bottom = feat[0:cols, :], feat[(rows - 1) * cols :, :]
    noise_top, noise_bottom = noise_coarse[0:w, :], noise_coarse[(h - 1) * w :, :]
    parts = [
        (top, noise_top),
        (bottom, noise_bottom),
        (
            get(s_fine, pl.ds(fine_stride + EDGE, rows, stride=fine_stride)),
            get(s_noise, pl.ds(stride + EDGE, h, stride=stride)),
        ),
        (
            get(s_fine, pl.ds(fine_stride + EDGE + cols - 1, rows, stride=fine_stride)),
            get(s_noise, pl.ds(stride + EDGE + w - 1, h, stride=stride)),
        ),
        (top[0:w], noise_top),
        (top[cols - w :], noise_top),
        (bottom[0:w], noise_bottom),
        (bottom[cols - w :], noise_bottom),
    ]
    enter()
    found = start(0, (cols + w, 2 * w), parts)

    for p, q in phases:
        for kr in range(2):
            for kc in range(2):
                total = None
                for a in TAPS[p][kr]:
                    for b in TAPS[q][kc]:
                        part = tap_of(w_prior, a, b).astype(F32)
                        total = part if total is None else total + part
                w_sums[((2 * p + kr) * 2 + q) * 2 + kc] = total.astype(BF16)

    def own(p):
        return slice(p * w, p * w + cells)

    put(mix, pl.ds(0, rows * cols), noise_fine[...])
    for p, q in phases:
        for i in range(h):
            fine[2 * p + q, (i + p) * w : (i + p + 1) * w, :] = get(
                mix, pl.ds((2 * i + p) * cols + q, w, stride=2)
            )

    def fill_feat(i, ms):
        p = i % 2
        at = (i - p) // 2 + p
        for m in ms:
            x_feat[p, m, at * w : (at + 1) * w, :] = get(
                s_fine, pl.ds((i + 1) * fine_stride + EDGE - 1 + m, w, stride=2)
            ).astype(BF16)

    for i in range(rows):
        fill_feat(i, (1, 2))
    finish(found)
    put(s_fine, pl.ds(EDGE, cols), halo(0, UP, 0, cols))
    put(s_fine, pl.ds((rows + 1) * fine_stride + EDGE, cols), halo(0, DOWN, 0, cols))
    put(s_fine, pl.ds(fine_stride + EDGE - 1, rows, stride=fine_stride), halo(0, LEFT, 0, rows))
    put(s_fine, pl.ds(fine_stride + EDGE + cols, rows, stride=fine_stride), halo(0, RIGHT, 0, rows))
    put(s_fine, pl.ds(EDGE - 1, 1), halo(0, UP_LEFT, 0, w)[w - 1 :])
    put(s_fine, pl.ds(EDGE + cols, 1), halo(0, UP_RIGHT, 0, w)[0:1])
    last = (rows + 1) * fine_stride + EDGE
    put(s_fine, pl.ds(last - 1, 1), halo(0, DOWN_LEFT, 0, w)[w - 1 :])
    put(s_fine, pl.ds(last + cols, 1), halo(0, DOWN_RIGHT, 0, w)[0:1])
    for i in range(rows):
        fill_feat(i, (0, 3))
    fill_feat(-1, (0, 1, 2, 3))
    fill_feat(rows, (0, 1, 2, 3))

    pooled = None
    for p, q in phases:
        total = None
        for a in range(3):
            for b in range(3):
                part = jnp.dot(
                    view(x_feat, p + a - 1, q + b - 1),
                    tap_of(w_post, a, b),
                    preferred_element_type=F32,
                )
                total = part if total is None else total + part
        total = total + fine[2 * p + q, own(p), :]
        fine[2 * p + q, own(p), :] = total
        pooled = total if pooled is None else pooled + total
    pooled = (0.25 * pooled).astype(BF16).astype(F32)
    for i in range(h):
        put(s_pool, pl.ds((i + 2) * stride + EDGE, w), pooled[i * w : (i + 1) * w])

    def line(p, q, i):
        return fine[2 * p + q, (i + p) * w : (i + p + 1) * w, :]

    def column(values, j):
        put(mix, pl.ds(0, cells), values)
        return get(mix, pl.ds(j, h, stride=w))

    pool_top, pool_bottom = pooled[0 : 2 * w], pooled[(h - 2) * w :]

    def pool_column(j):
        return get(s_pool, pl.ds(2 * stride + EDGE + j, h, stride=stride))

    lefts = [column(fine[2 * p, own(p), :], 0) for p in range(2)]
    rights = [column(fine[2 * p + 1, own(p), :], w - 1) for p in range(2)]
    parts = [
        (pool_top, line(0, 0, 0), line(0, 1, 0)),
        (pool_bottom, line(1, 0, h - 1), line(1, 1, h - 1)),
        (pool_column(0), pool_column(1), *lefts),
        (pool_column(w - 2), pool_column(w - 1), *rights),
        (pool_top, line(0, 0, 0)),
        (pool_top, line(0, 1, 0)),
        (pool_bottom, line(1, 0, h - 1)),
        (pool_bottom, line(1, 1, h - 1)),
    ]
    found = start(1, (4 * w, 3 * w), parts)
    for i in range(h):
        put(s_noise, pl.ds((i + 1) * stride + EDGE, w), noise_coarse[pl.ds(i * w, w), :])
    put(s_noise, pl.ds(EDGE, w), halo(0, UP, cols, w))
    put(s_noise, pl.ds((h + 1) * stride + EDGE, w), halo(0, DOWN, cols, w))
    put(s_noise, pl.ds(stride + EDGE - 1, h, stride=stride), halo(0, LEFT, rows, h))
    put(s_noise, pl.ds(stride + EDGE + w, h, stride=stride), halo(0, RIGHT, rows, h))
    put(s_noise, pl.ds(EDGE - 1, 1), halo(0, UP_LEFT, w, w)[w - 1 :])
    put(s_noise, pl.ds(EDGE + w, 1), halo(0, UP_RIGHT, w, w)[0:1])
    last = (h + 1) * stride + EDGE
    put(s_noise, pl.ds(last - 1, 1), halo(0, DOWN_LEFT, w, w)[w - 1 :])
    put(s_noise, pl.ds(last + w, 1), halo(0, DOWN_RIGHT, w, w)[0:1])
    finish(found)
    for k in range(2):
        put(s_pool, pl.ds(k * stride + EDGE, w), halo(1, UP, k * w, w))
        put(s_pool, pl.ds((h + 2 + k) * stride + EDGE, w), halo(1, DOWN, k * w, w))
        put(s_pool, pl.ds(2 * stride + EDGE - 2 + k, h, stride=stride), halo(1, LEFT, k * h, h))
        put(s_pool, pl.ds(2 * stride + EDGE + w + k, h, stride=stride), halo(1, RIGHT, k * h, h))
        put(s_pool, pl.ds(k * stride + EDGE - 2, 2), halo(1, UP_LEFT, k * w, w)[w - 2 :])
        put(s_pool, pl.ds(k * stride + EDGE + w, 2), halo(1, UP_RIGHT, k * w, w)[0:2])
        at = (h + 2 + k) * stride + EDGE
        put(s_pool, pl.ds(at - 2, 2), halo(1, DOWN_LEFT, k * w, w)[w - 2 :])
        put(s_pool, pl.ds(at + w, 2), halo(1, DOWN_RIGHT, k * w, w)[0:2])
    base = cells + w
    for q in range(2):
        fine[q, cells : cells + w, :] = halo(1, DOWN, (2 + q) * w, w)
        fine[2 + q, 0:w, :] = halo(1, UP, (2 + q) * w, w)
    for p in range(2):
        fine[2 * p, base + p : base + p + h, :] = halo(1, RIGHT, (2 + p) * h, h)
        fine[2 * p + 1, base + p : base + p + h, :] = halo(1, LEFT, (2 + p) * h, h)
    fine[3, base : base + 1, :] = halo(1, UP_LEFT, 2 * w, w)[w - 1 :]
    fine[2, base : base + 1, :] = halo(1, UP_RIGHT, 2 * w, w)[0:1]
    fine[1, base + h : base + h + 1, :] = halo(1, DOWN_LEFT, 2 * w, w)[w - 1 :]
    fine[0, base + h : base + h + 1, :] = halo(1, DOWN_RIGHT, 2 * w, w)[0:1]

    for i in range(h + 4):
        for b in range(3):
            x_pool[b, i * w : (i + 1) * w, :] = get(
                s_pool, pl.ds(i * stride + EDGE + b - 1, w)
            ).astype(BF16)
    for a in range(3):
        for b in range(3):
            both = [
                get(s_pool, pl.ds(a * stride + EDGE - 2 + b, side, stride=stride)),
                get(s_pool, pl.ds(a * stride + EDGE + w - 1 + b, side, stride=stride)),
            ]
            side_pool[3 * a + b] = jnp.concatenate(both, axis=0).astype(BF16)
    ring = (h + 2) * w
    noise = jnp.concatenate(
        [get(s_noise, pl.ds(i * stride + EDGE, w)) for i in range(h + 2)]
        + [
            get(s_noise, pl.ds(EDGE - 1, side, stride=stride)),
            get(s_noise, pl.ds(EDGE + w, side, stride=stride)),
        ],
        axis=0,
    )
    total = None
    for a in range(3):
        for b in range(3):
            x = jnp.concatenate([x_pool[b, pl.ds(a * w, ring), :], side_pool[3 * a + b]], axis=0)
            part = jnp.dot(x, tap_of(w_coarse, a, b), preferred_element_type=F32)
            total = part if total is None else total + part
    total = total + noise
    coarse[...] = total[w : w + cells]
    total = total.astype(BF16).astype(F32)
    put(s_ctx, pl.ds(EDGE, w), jnp.where(has_up, total[0:w], 0.0))
    for i in range(1, h + 1):
        put(s_ctx, pl.ds(i * stride + EDGE, w), total[i * w : (i + 1) * w])
    put(s_ctx, pl.ds((h + 1) * stride + EDGE, w), jnp.where(has_down, total[ring - w : ring], 0.0))
    place = lax.broadcasted_iota(jnp.int32, (side, chans), 0)
    first = jnp.where(has_up, 0, 1)
    limit = jnp.where(has_down, h + 2, h + 1)
    inside = jnp.logical_and(place >= first, place < limit)
    for at, has, values in (
        (EDGE - 1, has_left, total[ring : ring + side]),
        (EDGE + w, has_right, total[ring + side :]),
    ):
        put(
            s_ctx,
            pl.ds(at, side, stride=stride),
            jnp.where(jnp.logical_and(inside, has), values, 0.0),
        )
    for i in range(h + 2):
        for k in range(3):
            x_ctx[k, i * w : (i + 1) * w, :] = get(
                s_ctx, pl.ds(i * stride + EDGE + k - 1, w)
            ).astype(BF16)
    for q in range(2):
        for kr in range(2):
            for kc in range(2):
                at = kr * stride + EDGE + (w - 1 if q == 0 else -1) + kc
                side_ctx[(2 * q + kr) * 2 + kc] = get(
                    s_ctx, pl.ds(at, extra, stride=stride)
                ).astype(BF16)

    place = lax.broadcasted_iota(jnp.int32, (extra, 2 * chans), 0)
    for p, q in phases:
        prior = None
        for kr in range(2):
            for kc in range(2):
                x = jnp.concatenate(
                    [x_ctx[q + kc, pl.ds(kr * w, base), :], side_ctx[(2 * q + kr) * 2 + kc]],
                    axis=0,
                )
                part = jnp.dot(
                    x, w_sums[((2 * p + kr) * 2 + q) * 2 + kc], preferred_element_type=F32
                )
                prior = part if prior is None else prior + part
        raw = prior[:, chans:]
        small = jnp.exp(-jnp.abs(raw))
        sigma = jnp.maximum(raw, 0.0) + jnp.log1p(small) + 0.5
        gate = jnp.where(raw >= 0, 1.0, small) / (1.0 + small)
        inverse = 1.0 / sigma
        ratio = (fine[2 * p + q] - prior[:, :chans]) * inverse
        residual = ratio * inverse
        err[2 * p + q] = residual[own(p)]
        slope = (inverse - ratio * ratio * inverse) * gate
        both = jnp.concatenate([-residual, slope], axis=1).astype(BF16).astype(F32)
        if p == 0:
            g_main[q, 0:cells, :] = both[0:cells]
            g_main[q, cells:, :] = jnp.where(has_down, both[cells:base], 0.0)
            inside = jnp.logical_or(has_down, place < h)
        else:
            g_main[2 + q, 0:w, :] = jnp.where(has_up, both[0:w], 0.0)
            g_main[2 + q, w:, :] = both[w:base]
            inside = jnp.logical_or(has_up, place > 0)
        inside = jnp.logical_and(inside, has_left if q else has_right)
        g_side[2 * p + q] = jnp.where(inside, both[base:], 0.0)

    windows = ((1, 1), (0, 1), (0, 0))
    for a in range(3):
        i0, i1 = windows[a]
        for q in range(2):
            total = g_main[q, pl.ds(i0 * w, cells), :] + g_main[2 + q, pl.ds(i1 * w, cells), :]
            for i in range(h):
                put(s_pair.at[q], pl.ds(i * stride + EDGE, w), total[i * w : (i + 1) * w])
            total = g_side[q, i0 : i0 + h, :] + g_side[2 + q, i1 : i1 + h, :]
            put(s_pair.at[q], pl.ds(EDGE - 1 if q else EDGE + w, h, stride=stride), total)
        for i in range(h):
            at = i * stride + EDGE
            even, odd = get(s_pair.at[0], pl.ds(at, w)), get(s_pair.at[1], pl.ds(at, w))
            here = slice(i * w, (i + 1) * w)
            boxes[3 * a, here, :] = (odd + get(s_pair.at[0], pl.ds(at + 1, w))).astype(BF16)
            boxes[3 * a + 1, here, :] = (even + odd).astype(BF16)
            boxes[3 * a + 2, here, :] = (get(s_pair.at[1], pl.ds(at - 1, w)) + even).astype(BF16)

    for tap in range(9):
        spread(
            parts_prior,
            tap * chans,
            scale * dot_in(x_ctx[1, pl.ds(w, cells), :], boxes[tap]),
        )
    prior_1()
    prior_2()
    total = None
    for tap in range(9):
        part = dot_out(boxes[tap], tap_of(w_prior, tap // 3, tap % 3))
        total = part if total is None else total + part
    total = (coarse[...] + total).astype(BF16).astype(F32)

    def pad_lines(values):
        for i in range(h):
            put(s_pool, pl.ds((i + 1) * stride + EDGE, w), values[i * w : (i + 1) * w])

    pad_lines(total)
    parts = [
        (total[0:w],),
        (total[cells - w :],),
        (get(s_pool, pl.ds(stride + EDGE, h, stride=stride)),),
        (get(s_pool, pl.ds(stride + EDGE + w - 1, h, stride=stride)),),
        (total[0:w],),
        (total[0:w],),
        (total[cells - w :],),
        (total[cells - w :],),
    ]
    found = start(2, (w, w), parts)
    gco = total.astype(BF16)
    for a in range(3):
        for b in range(3):
            spread(
                parts_coarse,
                (3 * a + b) * chans,
                scale * dot_in(x_pool[b, pl.ds((a + 1) * w, cells), :], gco),
            )
    middle()
    prior_1()
    prior_2()
    finish(found)

    put(s_pool, pl.ds(EDGE, w), halo(2, UP, 0, w))
    put(s_pool, pl.ds((h + 1) * stride + EDGE, w), halo(2, DOWN, 0, w))
    put(s_pool, pl.ds(stride + EDGE - 1, h, stride=stride), halo(2, LEFT, 0, h))
    put(s_pool, pl.ds(stride + EDGE + w, h, stride=stride), halo(2, RIGHT, 0, h))
    put(s_pool, pl.ds(EDGE - 1, 1), halo(2, UP_LEFT, 0, w)[w - 1 :])
    put(s_pool, pl.ds(EDGE + w, 1), halo(2, UP_RIGHT, 0, w)[0:1])
    last = (h + 1) * stride + EDGE
    put(s_pool, pl.ds(last - 1, 1), halo(2, DOWN_LEFT, 0, w)[w - 1 :])
    put(s_pool, pl.ds(last + w, 1), halo(2, DOWN_RIGHT, 0, w)[0:1])
    for i in range(h + 2):
        for k in range(3):
            x_gco[k, i * w : (i + 1) * w, :] = get(
                s_pool, pl.ds(i * stride + EDGE + k - 1, w)
            ).astype(BF16)
    total = None
    for a in range(3):
        for b in range(3):
            part = dot_out(x_gco[2 - b, pl.ds((2 - a) * w, cells), :], tap_of(w_coarse, a, b))
            total = part if total is None else total + part
    total = 0.25 * total

    for p, q in phases:
        own_gfi[2 * p + q] = (err[2 * p + q] + total).astype(BF16)

    def s_gfi(q):
        return s_pair.at[q, pl.ds(0, chans // LANES)]

    def gfi_line(p, q, i):
        return own_gfi[2 * p + q, i * w : (i + 1) * w, :]

    for p, q in phases:
        for i in range(h):
            put(
                s_gfi(q),
                pl.ds((i + p * h) * stride + EDGE, w),
                own_gfi[2 * p + q, i * w : (i + 1) * w, :].astype(F32),
            )

    def gfi_column(p, q):
        at = p * h * stride + EDGE + (w - 1 if q else 0)
        return get(s_gfi(q), pl.ds(at, h, stride=stride))

    parts = [
        (gfi_line(0, 0, 0), gfi_line(0, 1, 0)),
        (gfi_line(1, 0, h - 1), gfi_line(1, 1, h - 1)),
        (gfi_column(0, 0), gfi_column(1, 0)),
        (gfi_column(0, 1), gfi_column(1, 1)),
        (gfi_line(0, 0, 0),),
        (gfi_line(0, 1, 0),),
        (gfi_line(1, 0, h - 1),),
        (gfi_line(1, 1, h - 1),),
    ]
    found = start(3, (2 * w, w), parts)
    for a in range(3):
        for b in range(3):
            total = None
            for p, q in phases:
                part = dot_in(view(x_feat, p + a - 1, q + b - 1), own_gfi[2 * p + q])
                total = part if total is None else total + part
            spread(parts_post, (3 * a + b) * chans, scale * total)
    post_1()
    post_2()
    middle()
    prior_1()
    prior_2()
    finish(found)
    for p in range(2):
        put(s_gfi(1), pl.ds(p * h * stride + EDGE - 1, h, stride=stride), halo(3, LEFT, p * h, h))
        put(s_gfi(0), pl.ds(p * h * stride + EDGE + w, h, stride=stride), halo(3, RIGHT, p * h, h))
        for q in range(2):
            x_gfi[p, 1 + q, p * w : p * w + cells, :] = own_gfi[2 * p + q]
            x_gfi[p, 1 + q, (1 - p) * cells : (1 - p) * cells + w, :] = halos[
                3, UP if p else DOWN, q * w : (q + 1) * w, :
            ]
        for i in range(h):
            here = slice((i + p) * w, (i + p + 1) * w)
            at = (i + p * h) * stride + EDGE
            x_gfi[p, 0, here, :] = get(s_gfi(1), pl.ds(at - 1, w)).astype(BF16)
            x_gfi[p, 3, here, :] = get(s_gfi(0), pl.ds(at + 1, w)).astype(BF16)
        ring_at = slice((1 - p) * cells, (1 - p) * cells + w)
        vertical_side = UP if p else DOWN
        left = halo(3, UP_LEFT if p else DOWN_LEFT, 0, w)[w - 1 :]
        right = halo(3, UP_RIGHT if p else DOWN_RIGHT, 0, w)[0:1]
        put(s_gfi(1), pl.ds(EDGE - 1, 1), left)
        put(s_gfi(1), pl.ds(EDGE, w), halo(3, vertical_side, w, w))
        put(s_gfi(0), pl.ds(EDGE, w), halo(3, vertical_side, 0, w))
        put(s_gfi(0), pl.ds(EDGE + w, 1), right)
        x_gfi[p, 0, ring_at, :] = get(s_gfi(1), pl.ds(EDGE - 1, w)).astype(BF16)
        x_gfi[p, 3, ring_at, :] = get(s_gfi(0), pl.ds(EDGE + 1, w)).astype(BF16)
    post_1()
    post_2()
    for p, q in phases:
        total = None
        for a in range(3):
            for b in range(3):
                part = dot_out(view(x_gfi, p - a + 1, q - b + 1), tap_of(w_post, a, b))
                total = part if total is None else total + part
        for i in range(h):
            put(mix, pl.ds((2 * i + p) * cols + q, w, stride=2), total[i * w : (i + 1) * w])
    grad_feat[...] = get(mix, pl.ds(0, rows * cols)).astype(BF16)
    for _ in range(bits + 1):
        for step in (prior_1, prior_2, middle, post_1, post_2):
            step()


def hand_out(*refs):
    for source, target in zip(refs[:4], refs[4:]):
        target[...] = source[...]


def on_device(sizes, feat, noise_fine, noise_coarse, w_post, w_coarse, w_prior):
    n_row, n_col = sizes
    rows, cols, chans = feat.shape
    h, w = rows // 2, cols // 2
    scale = 1.0 / math.sqrt(rows * n_row * cols * n_col)
    cells, quarter = rows * cols, h * w
    vmem = pl.BlockSpec(memory_space=pltpu.VMEM)
    dims = (rows, cols, chans, scale, n_row, n_col)
    count = n_row * n_col
    per = w_post.shape[0] // count
    widths = (chans // 2, chans // 2, chans, chans, chans)
    extra, side, stride = round_up(h + 1, 16), round_up(h + 2, 8), w + 2 * EDGE

    def lanes(n, depth=chans):
        return pltpu.VMEM((depth // LANES, n, LANES), F32)

    grad_feat, out_post, out_coarse, out_prior = pl.pallas_call(
        functools.partial(tile_kernel, dims),
        out_shape=(
            jax.ShapeDtypeStruct((cells, chans), BF16),
            jax.ShapeDtypeStruct((per * chans // LANES, LANES), F32),
            jax.ShapeDtypeStruct((per * chans // LANES, LANES), F32),
            jax.ShapeDtypeStruct((per * 2 * chans // LANES, LANES), F32),
        ),
        in_specs=[vmem] * 6,
        out_specs=(vmem,) * 4,
        scratch_shapes=[
            pltpu.VMEM((4, (h + 1) * w + extra, chans), F32),
            pltpu.VMEM((4, quarter, chans), F32),
            pltpu.VMEM((quarter, chans), F32),
            lanes((rows + 2) * (cols + 2 * EDGE)),
            lanes((side + 2) * stride),
            lanes(side * stride),
            lanes((extra + 1) * stride),
            pltpu.VMEM((2, 2 * chans // LANES, max(2 * h * stride, cells), LANES), F32),
            pltpu.VMEM((2, 4, (h + 1) * w, chans), BF16),
            pltpu.VMEM((3, (h + 4) * w, chans), BF16),
            pltpu.VMEM((9, 2 * side, chans), BF16),
            pltpu.VMEM((3, (h + 2) * w, chans), BF16),
            pltpu.VMEM((8, extra, chans), BF16),
            pltpu.VMEM((16, chans, 2 * chans), BF16),
            pltpu.VMEM((4, (h + 1) * w, 2 * chans), F32),
            pltpu.VMEM((4, extra, 2 * chans), F32),
            pltpu.VMEM((9, quarter, 2 * chans), BF16),
            pltpu.VMEM((4, quarter, chans), BF16),
            pltpu.VMEM((4, 8, 4 * w, chans), BF16),
            pltpu.VMEM((4, 8, 4 * w, chans), BF16),
            [pltpu.VMEM((count, per, width), F32) for width in widths],
            [pltpu.VMEM((count // 2, per, width), BF16) for width in widths],
            [pltpu.VMEM((count - 1, per, width), BF16) for width in widths],
            pltpu.SemaphoreType.DMA((4, 16)),
            pltpu.SemaphoreType.DMA((5, count.bit_length() - 1, 2)),
        ],
        compiler_params=pltpu.CompilerParams(
            collective_id=0, has_side_effects=True, vmem_limit_bytes=65000 * 1024
        ),
    )(
        feat.reshape(cells, chans),
        noise_fine.reshape(cells, chans),
        noise_coarse.reshape(quarter, chans),
        w_post,
        w_coarse,
        w_prior,
    )
    results = (grad_feat, out_post, out_coarse, out_prior)
    grad_feat, out_post, out_coarse, out_prior = pl.pallas_call(
        hand_out,
        out_shape=tuple(jax.ShapeDtypeStruct(a.shape, a.dtype) for a in results),
        in_specs=[vmem] * 4,
        out_specs=(vmem,) * 4,
    )(*results)
    return (
        grad_feat.reshape(rows, cols, chans),
        out_post.reshape(-1),
        out_coarse.reshape(-1),
        out_prior.reshape(-1),
    )


def solution(mesh):
    sizes = (mesh.shape["row"], mesh.shape["col"])
    return jax.shard_map(
        functools.partial(on_device, sizes),
        mesh=mesh,
        in_specs=(
            P("row", "col", None),
            P("row", "col", None),
            P("row", "col", None),
            P(),
            P(),
            P(),
        ),
        out_specs=(P("row", "col", None), P(("row", "col")), P(("row", "col")), P(("row", "col"))),
        check_vma=False,
    )
```

time: 84.5 us -> 59.4 us (0.70)
  Pallas kernels: 83.8 us -> 58.6 us
    pallas_call x1, Pallas kernels: 81.7 us -> 56.6 us  [on_device(): pl.pallas_call(functools.partial(tile_kernel, dims), out_shape=(jax.Shape...]
where the time goes in v1:
time: 59.4 us; the launch traced here: 59.2 us
  Pallas kernels  58.6 us (99%)
  between operations  0.64 us (1%)
    pallas_call x1, Pallas kernels, on_device(): pl.pallas_call(functools.partial(tile_kernel, dims), out_shape=(jax.Shape...  56.6 us
    pallas_call x1, Pallas kernels, on_device(): pl.pallas_call(hand_out, out_shape=tuple((jax.ShapeDtypeStruct(a.shape, a...  2.03 us

profile of v1, /device:TPU:0, one launch (start us, length us, event | category | flops | bytes accessed | tf_op | source)
XLA Modules:
  0.0 59.2 jit_solution(14937756645043815330)
XLA Ops:
  0.6 56.6 %shard_map.93 = (bf16[1024,256]{1,0:T(8,128)(2,1)}, f32[144,128]{1,0:T(8,128)}, f32[144,128]{1,0:T(8,128)}, f32[288,128]{1,0:T(8,128)}) custom-call(bf16[1024,256]{1,0:T(8,128)(2,1)} %bitcast.8, f32[1024,256]{1,0:T(8,128)} %bitcast.7, f32[256,256]{1,0:T(8,128)} %bitcast.9, bf16[2304,256]{1,0:T(8,128)(2,1)} %w_post.1, bf16[2304,256]{1,0:T(8,128)(2,1)} %w_coarse.1, ...), custom_call_target="tpu_custom_call" | custom-call | tf_op jit(solution)/shard_map/pallas_call | solution.py:720
  57.2 2.0 %shard_map.94 = (bf16[1024,256]{1,0:T(8,128)(2,1)}, f32[144,128]{1,0:T(8,128)}, f32[144,128]{1,0:T(8,128)}, f32[288,128]{1,0:T(8,128)}) custom-call(bf16[1024,256]{1,0:T(8,128)(2,1)} %get-tuple-element.12.refs_0_, f32[144,128]{1,0:T(8,128)} %get-tuple-element.13.refs_1_, f32[144,128]{1,0:T(8,128)} %get-tuple-element.14.refs_2_, ...), custom_call_target="tpu_custom_call" | custom-call | tf_op jit(solution)/shard_map/pallas_call | solution.py:769

commit v2 on v1

--- a/solution.py
+++ b/solution.py
@@ -28,6 +28,7 @@
 DIRECTIONS = ((-1, 0), (1, 0), (0, -1), (0, 1), (-1, -1), (-1, 1), (1, -1), (1, 1))
 OPPOSITE = (1, 0, 3, 2, 7, 6, 5, 4)
 UP, DOWN, LEFT, RIGHT, UP_LEFT, UP_RIGHT, DOWN_LEFT, DOWN_RIGHT = range(8)
+CORNER = 16
 TAPS = (((0,), (1, 2)), ((0, 1), (2,)))
 
 
@@ -37,44 +38,61 @@
 
 def tile_kernel(
     dims,
-    feat,
-    noise_fine,
-    noise_coarse,
-    w_post,
-    w_coarse,
-    w_prior,
-    grad_feat,
-    out_post,
-    out_coarse,
-    out_prior,
-    fine,
-    err,
-    coarse,
-    s_fine,
-    s_pool,
-    s_noise,
-    s_ctx,
-    s_pair,
-    x_feat,
-    x_pool,
-    side_pool,
-    x_ctx,
-    side_ctx,
-    w_sums,
-    g_main,
-    g_side,
-    boxes,
-    own_gfi,
-    edges,
-    halos,
-    sums,
-    outgoing,
-    incoming,
-    sems,
-    chain_sems,
+    *refs,
 ):
+    operands, results = refs[:6], refs[6:10]
+    (
+        feat,
+        noise_fine,
+        noise_coarse,
+        w_post,
+        w_coarse,
+        w_prior,
+        grad_feat,
+        out_post,
+        out_coarse,
+        out_prior,
+        fine,
+        err,
+        coarse,
+        s_fine,
+        s_pool,
+        s_noise,
+        s_ctx,
+        s_pair,
+        s_corner,
+        x_feat,
+        x_pool,
+        side_pool,
+        x_ctx,
+        side_ctx,
+        w_sums,
+        g_main,
+        g_side,
+        boxes,
+        own_gfi,
+        edges,
+        halos,
+        sums,
+        outgoing,
+        incoming,
+        sems,
+        chain_sems,
+        load_sems,
+        store_sems,
+    ) = refs[10:]
+    loads = [
+        pltpu.make_async_copy(source, target, load_sems.at[k])
+        for k, (source, target) in enumerate(zip(operands, refs[10:16]))
+    ]
+    stores = [
+        pltpu.make_async_copy(source, target, store_sems.at[k])
+        for k, (source, target) in enumerate(zip(refs[16:20], results))
+    ]
+    for k in (0, 2, 5, 1, 3, 4):
+        loads[k].start()
     x_gco, x_gfi = x_ctx, x_feat
-    rows, cols, chans, scale, n_row, n_col = dims
+    rows, cols, chans, scale, n_row, n_col, orders = dims
     mix = s_pair.at[0, pl.ds(0, chans // LANES)]
     h, w = rows // 2, cols // 2
     cells = h * w
@@ -116,21 +134,32 @@
     def bit_of(b):
         return me // 2**b % 2
 
-    def partner(b):
-        if b < col_bits:
-            return {"col": c + 2**b * (1 - 2 * bit_of(b))}
-        return {"row": r + 2 ** (b - col_bits) * (1 - 2 * bit_of(b))}
-
-    for b in range(bits):
+    def reach(group, mask):
+        row, col = r, c
+        for q, b in enumerate(group):
+            if mask >> q & 1:
+                if b < col_bits:
+                    col = col + 2**b * (1 - 2 * bit_of(b))
+                else:
+                    row = row + 2 ** (b - col_bits) * (1 - 2 * bit_of(b))
+        return {"row": row, "col": col}
+
+    partners = {}
+    for order in orders:
+        for group in order:
+            for mask in range(1, 2 ** len(group)):
+                flips = tuple(b for q, b in enumerate(group) if mask >> q & 1)
+                partners[flips] = reach(group, mask)
+    for device in partners.values():
         pl.semaphore_signal(
-            barrier, inc=1, device_id=partner(b), device_id_type=pl.DeviceIdType.MESH
+            barrier, inc=1, device_id=device, device_id_type=pl.DeviceIdType.MESH
         )
 
-    for ref in (s_fine, s_pool, s_noise, s_ctx, fine):
+    for ref in (s_fine, s_pool, s_noise, s_ctx, s_corner, fine):
         ref[...] = jnp.zeros_like(ref)
 
     def enter():
-        pl.semaphore_wait(barrier, bits + sum(has.astype(jnp.int32) for has, _device in sides))
+        pl.semaphore_wait(barrier, len(partners) + sum(has.astype(jnp.int32) for has, _device in sides))
 
     def each(n, body):
         if n <= 16:
@@ -141,20 +170,28 @@
 
     def chain(number, order, out, out_at):
         acc, send, recv = sums[number], outgoing[number], incoming[number]
-        state = {"step": 0, "copy": None}
-
-        def offset(k):
-            return count - (count >> k)
+        state = {"step": 0, "copies": []}
+        frees = [[b for b in range(bits) if b not in sum(order[:k], ())] for k in range(len(order) + 1)]
+        lefts = [2 ** len(free) for free in frees]
+        bases = [count - left for left in lefts]
+
+        def arrived(k, slot):
+            total = None
+            for mask in range(1, 2 ** len(order[k])):
+                part = recv[bases[k] + (mask - 1) * lefts[k + 1] + slot].astype(F32)
+                total = part if total is None else total + part
+            return total
 
         def step():
             k = state["step"]
-            if k > bits:
+            if k > len(order):
                 return
             state["step"] = k + 1
-            if k > 0:
-                state["copy"].wait()
-            if k == bits:
-                total = acc[me] + recv[offset(k - 1)].astype(F32)
+            for copy in state["copies"]:
+                copy.wait()
+            state["copies"] = []
+            if k == len(order):
+                total = scale * (acc[me] + arrived(k - 1, 0))
                 per = total.shape[0]
                 stride = out.shape[0] // per
                 for d in range(total.shape[1] // LANES):
@@ -162,39 +199,45 @@
                         :, d * LANES : (d + 1) * LANES
                     ]
                 return
-            bit = order[k]
-            free = [b for b in range(bits) if b not in order[:k]]
-            rest = [b for b in free if b != bit]
-            place = free.index(bit)
-            fixed = sum((bit_of(b) * 2**b for b in order[:k]), 0)
-            n = count >> (k + 1)
-
-            def value(j, choice):
-                index = fixed + choice * 2**bit
-                for q, b in enumerate(rest):
-                    index = index + j // 2**q % 2 * 2**b
+            group, free, n = order[k], frees[k], lefts[k + 1]
+            rest = frees[k + 1]
+            fixed = sum((bit_of(b) * 2**b for b in range(bits) if b not in free), 0)
+
+            def value(j, mask):
+                index, slot = fixed, 0
+                for q, b in enumerate(free):
+                    if b in group:
+                        flip = mask >> group.index(b) & 1
+                        bit = 1 - bit_of(b) if flip else bit_of(b)
+                    else:
+                        bit = j // 2 ** rest.index(b) % 2
+                    index = index + bit * 2**b
+                    slot = slot + bit * 2**q
                 total = acc[index]
                 if k > 0:
-                    slot = j // 2**place * 2 ** (place + 1) + choice * 2**place + j % 2**place
-                    total = total + recv[offset(k - 1) + slot].astype(F32)
+                    total = total + arrived(k - 1, slot)
                 return index, total
 
-            def fill(j):
-                send[j] = value(j, 1 - bit_of(bit))[1].astype(BF16)
-
-            each(n, fill)
-            state["copy"] = pltpu.make_async_remote_copy(
-                src_ref=send.at[pl.ds(0, n)],
-                dst_ref=recv.at[pl.ds(offset(k), n)],
-                send_sem=chain_sems.at[number, k, 0],
-                recv_sem=chain_sems.at[number, k, 1],
-                device_id=partner(bit),
-                device_id_type=pl.DeviceIdType.MESH,
-            )
-            state["copy"].start()
+            for mask in reversed(range(1, 2 ** len(group))):
+                at = (mask - 1) * n
+
+                def fill(j, mask=mask, at=at):
+                    send[at + j] = value(j, mask)[1].astype(BF16)
+
+                each(n, fill)
+                copy = pltpu.make_async_remote_copy(
+                    src_ref=send.at[pl.ds(at, n)],
+                    dst_ref=recv.at[pl.ds(bases[k] + at, n)],
+                    send_sem=chain_sems.at[number, k, mask - 1, 0],
+                    recv_sem=chain_sems.at[number, k, mask - 1, 1],
+                    device_id=reach(group, mask),
+                    device_id_type=pl.DeviceIdType.MESH,
+                )
+                copy.start()
+                state["copies"].append(copy)
 
             def keep(j):
-                index, total = value(j, bit_of(bit))
+                index, total = value(j, 0)
                 acc[index] = total
 
             if k > 0:
@@ -203,19 +246,23 @@
         return step
 
 
-    near, rest = [0], list(range(1, bits))
-    first = near + rest
-    second = near + rest[1::-1] + rest[2:]
-    third = near + rest[2:3] + rest[:2] + rest[3:]
-    half = chans // 2
-    post_1 = chain(0, first, out_post, 0)
-    post_2 = chain(1, second, out_post, half)
-    middle = chain(2, third, out_coarse, 0)
-    prior_1 = chain(3, first, out_prior, 0)
-    prior_2 = chain(4, second, out_prior, chans)
-    parts_post = ((sums[0], 0), (sums[1], half))
-    parts_coarse = ((sums[2], 0),)
-    parts_prior = ((sums[3], 0), (sums[4], chans))
+    pieces = chans // LANES
+    post_chains = [chain(k, orders[k], out_post, k * LANES) for k in range(pieces)]
+    middle_chains = [chain(k, orders[k], out_coarse, (k - pieces) * LANES) for k in range(pieces, 2 * pieces)]
+    prior_chains = [
+        chain(k, orders[k], out_prior, (k - 2 * pieces) * LANES)
+        for k in range(2 * pieces, 4 * pieces)
+    ]
+
+    early, late = prior_chains[:2], prior_chains[2:]
+
+    def advance(chains):
+        for step in chains:
+            step()
+
+    parts_post = [(sums[k], k * LANES) for k in range(pieces)]
+    parts_coarse = [(sums[k + pieces], k * LANES) for k in range(pieces)]
+    parts_prior = [(sums[2 * pieces + k], k % pieces * LANES) for k in range(2 * pieces)]
 
     def spread(parts, start, values):
         height = values.shape[0]
@@ -267,6 +314,13 @@
     def halo(index, d, at, size):
         return halos[index, d, at : at + size, :].astype(F32)
 
+    def corner(k, *pieces):
+        at = k * CORNER
+        for piece in pieces:
+            put(s_corner, pl.ds(at, piece.shape[0]), piece)
+            at += piece.shape[0]
+        return (get(s_corner, pl.ds(k * CORNER, CORNER)),)
+
     def view(x, t, u):
         return x[t % 2, u + 1, pl.ds(w if t >= 1 else 0, cells), :]
 
@@ -286,6 +340,8 @@
     side = round_up(h + 2, 8)
     phases = [(p, q) for p in range(2) for q in range(2)]
 
+    loads[0].wait()
+    loads[2].wait()
     for i in range(rows):
         put(
             s_fine,
@@ -307,14 +363,16 @@
             get(s_fine, pl.ds(fine_stride + EDGE + cols - 1, rows, stride=fine_stride)),
             get(s_noise, pl.ds(stride + EDGE + w - 1, h, stride=stride)),
         ),
-        (top[0:w], noise_top),
-        (top[cols - w :], noise_top),
-        (bottom[0:w], noise_bottom),
-        (bottom[cols - w :], noise_bottom),
     ]
+    for k in range(4):
+        i, j = k // 2, k % 2
+        at = (i * (rows - 1) + 1) * fine_stride + EDGE + j * (cols - 1)
+        noise_at = (i * (h - 1) + 1) * stride + EDGE + j * (w - 1)
+        parts.append(corner(k, get(s_fine, pl.ds(at, 1)), get(s_noise, pl.ds(noise_at, 1))))
     enter()
-    found = start(0, (cols + w, 2 * w), parts)
-
+    found = start(0, (cols + w, CORNER), parts)
+
+    loads[5].wait()
     for p, q in phases:
         for kr in range(2):
             for kc in range(2):
@@ -328,6 +386,7 @@
     def own(p):
         return slice(p * w, p * w + cells)
 
+    loads[1].wait()
     put(mix, pl.ds(0, rows * cols), noise_fine[...])
     for p, q in phases:
         for i in range(h):
@@ -345,16 +404,28 @@
 
     for i in range(rows):
         fill_feat(i, (1, 2))
+    def dot_fine(p, q, a, b):
+        x = view(x_feat, p + a - 1, q + b - 1)
+        return jnp.dot(x, tap_of(w_post, a, b), preferred_element_type=F32)
+
+    loads[3].wait()
+    for p, q in phases:
+        total = None
+        for a in range(1 - p, 3 - p):
+            for b in range(1 - q, 3 - q):
+                part = dot_fine(p, q, a, b)
+                total = part if total is None else total + part
+        fine[2 * p + q, own(p), :] = total + fine[2 * p + q, own(p), :]
     finish(found)
     put(s_fine, pl.ds(EDGE, cols), halo(0, UP, 0, cols))
     put(s_fine, pl.ds((rows + 1) * fine_stride + EDGE, cols), halo(0, DOWN, 0, cols))
     put(s_fine, pl.ds(fine_stride + EDGE - 1, rows, stride=fine_stride), halo(0, LEFT, 0, rows))
     put(s_fine, pl.ds(fine_stride + EDGE + cols, rows, stride=fine_stride), halo(0, RIGHT, 0, rows))
-    put(s_fine, pl.ds(EDGE - 1, 1), halo(0, UP_LEFT, 0, w)[w - 1 :])
-    put(s_fine, pl.ds(EDGE + cols, 1), halo(0, UP_RIGHT, 0, w)[0:1])
+    put(s_fine, pl.ds(EDGE - 1, 1), halo(0, UP_LEFT, 0, CORNER)[0:1])
+    put(s_fine, pl.ds(EDGE + cols, 1), halo(0, UP_RIGHT, 0, CORNER)[0:1])
     last = (rows + 1) * fine_stride + EDGE
-    put(s_fine, pl.ds(last - 1, 1), halo(0, DOWN_LEFT, 0, w)[w - 1 :])
-    put(s_fine, pl.ds(last + cols, 1), halo(0, DOWN_RIGHT, 0, w)[0:1])
+    put(s_fine, pl.ds(last - 1, 1), halo(0, DOWN_LEFT, 0, CORNER)[0:1])
+    put(s_fine, pl.ds(last + cols, 1), halo(0, DOWN_RIGHT, 0, CORNER)[0:1])
     for i in range(rows):
         fill_feat(i, (0, 3))
     fill_feat(-1, (0, 1, 2, 3))
@@ -365,11 +436,9 @@
         total = None
         for a in range(3):
             for b in range(3):
-                part = jnp.dot(
-                    view(x_feat, p + a - 1, q + b - 1),
-                    tap_of(w_post, a, b),
-                    preferred_element_type=F32,
-                )
+                if p + a - 1 in (0, 1) and q + b - 1 in (0, 1):
+                    continue
+                part = dot_fine(p, q, a, b)
                 total = part if total is None else total + part
         total = total + fine[2 * p + q, own(p), :]
         fine[2 * p + q, own(p), :] = total
@@ -397,34 +466,37 @@
         (pool_bottom, line(1, 0, h - 1), line(1, 1, h - 1)),
         (pool_column(0), pool_column(1), *lefts),
         (pool_column(w - 2), pool_column(w - 1), *rights),
-        (pool_top, line(0, 0, 0)),
-        (pool_top, line(0, 1, 0)),
-        (pool_bottom, line(1, 0, h - 1)),
-        (pool_bottom, line(1, 1, h - 1)),
     ]
-    found = start(1, (4 * w, 3 * w), parts)
+    for k in range(4):
+        i, j = k // 2, k % 2
+        at = (i * (h - 2) + 2) * stride + EDGE + j * (w - 2)
+        cell = line(i, j, i * (h - 1))[j * (w - 1) : j * (w - 1) + 1]
+        parts.append(
+            corner(k, get(s_pool, pl.ds(at, 2)), get(s_pool, pl.ds(at + stride, 2)), cell)
+        )
+    found = start(1, (4 * w, CORNER), parts)
     for i in range(h):
         put(s_noise, pl.ds((i + 1) * stride + EDGE, w), noise_coarse[pl.ds(i * w, w), :])
     put(s_noise, pl.ds(EDGE, w), halo(0, UP, cols, w))
     put(s_noise, pl.ds((h + 1) * stride + EDGE, w), halo(0, DOWN, cols, w))
     put(s_noise, pl.ds(stride + EDGE - 1, h, stride=stride), halo(0, LEFT, rows, h))
     put(s_noise, pl.ds(stride + EDGE + w, h, stride=stride), halo(0, RIGHT, rows, h))
-    put(s_noise, pl.ds(EDGE - 1, 1), halo(0, UP_LEFT, w, w)[w - 1 :])
-    put(s_noise, pl.ds(EDGE + w, 1), halo(0, UP_RIGHT, w, w)[0:1])
+    put(s_noise, pl.ds(EDGE - 1, 1), halo(0, UP_LEFT, 0, CORNER)[1:2])
+    put(s_noise, pl.ds(EDGE + w, 1), halo(0, UP_RIGHT, 0, CORNER)[1:2])
     last = (h + 1) * stride + EDGE
-    put(s_noise, pl.ds(last - 1, 1), halo(0, DOWN_LEFT, w, w)[w - 1 :])
-    put(s_noise, pl.ds(last + w, 1), halo(0, DOWN_RIGHT, w, w)[0:1])
+    put(s_noise, pl.ds(last - 1, 1), halo(0, DOWN_LEFT, 0, CORNER)[1:2])
+    put(s_noise, pl.ds(last + w, 1), halo(0, DOWN_RIGHT, 0, CORNER)[1:2])
     finish(found)
     for k in range(2):
         put(s_pool, pl.ds(k * stride + EDGE, w), halo(1, UP, k * w, w))
         put(s_pool, pl.ds((h + 2 + k) * stride + EDGE, w), halo(1, DOWN, k * w, w))
         put(s_pool, pl.ds(2 * stride + EDGE - 2 + k, h, stride=stride), halo(1, LEFT, k * h, h))
         put(s_pool, pl.ds(2 * stride + EDGE + w + k, h, stride=stride), halo(1, RIGHT, k * h, h))
-        put(s_pool, pl.ds(k * stride + EDGE - 2, 2), halo(1, UP_LEFT, k * w, w)[w - 2 :])
-        put(s_pool, pl.ds(k * stride + EDGE + w, 2), halo(1, UP_RIGHT, k * w, w)[0:2])
+        put(s_pool, pl.ds(k * stride + EDGE - 2, 2), halo(1, UP_LEFT, 0, CORNER)[2 * k : 2 * k + 2])
+        put(s_pool, pl.ds(k * stride + EDGE + w, 2), halo(1, UP_RIGHT, 0, CORNER)[2 * k : 2 * k + 2])
         at = (h + 2 + k) * stride + EDGE
-        put(s_pool, pl.ds(at - 2, 2), halo(1, DOWN_LEFT, k * w, w)[w - 2 :])
-        put(s_pool, pl.ds(at + w, 2), halo(1, DOWN_RIGHT, k * w, w)[0:2])
+        put(s_pool, pl.ds(at - 2, 2), halo(1, DOWN_LEFT, 0, CORNER)[2 * k : 2 * k + 2])
+        put(s_pool, pl.ds(at + w, 2), halo(1, DOWN_RIGHT, 0, CORNER)[2 * k : 2 * k + 2])
     base = cells + w
     for q in range(2):
         fine[q, cells : cells + w, :] = halo(1, DOWN, (2 + q) * w, w)
@@ -432,11 +504,12 @@
     for p in range(2):
         fine[2 * p, base + p : base + p + h, :] = halo(1, RIGHT, (2 + p) * h, h)
         fine[2 * p + 1, base + p : base + p + h, :] = halo(1, LEFT, (2 + p) * h, h)
-    fine[3, base : base + 1, :] = halo(1, UP_LEFT, 2 * w, w)[w - 1 :]
-    fine[2, base : base + 1, :] = halo(1, UP_RIGHT, 2 * w, w)[0:1]
-    fine[1, base + h : base + h + 1, :] = halo(1, DOWN_LEFT, 2 * w, w)[w - 1 :]
-    fine[0, base + h : base + h + 1, :] = halo(1, DOWN_RIGHT, 2 * w, w)[0:1]
-
+    fine[3, base : base + 1, :] = halo(1, UP_LEFT, 0, CORNER)[4:5]
+    fine[2, base : base + 1, :] = halo(1, UP_RIGHT, 0, CORNER)[4:5]
+    fine[1, base + h : base + h + 1, :] = halo(1, DOWN_LEFT, 0, CORNER)[4:5]
+    fine[0, base + h : base + h + 1, :] = halo(1, DOWN_RIGHT, 0, CORNER)[4:5]
+
+    loads[4].wait()
     for i in range(h + 4):
         for b in range(3):
             x_pool[b, i * w : (i + 1) * w, :] = get(
@@ -548,14 +621,6 @@
             boxes[3 * a + 1, here, :] = (even + odd).astype(BF16)
             boxes[3 * a + 2, here, :] = (get(s_pair.at[1], pl.ds(at - 1, w)) + even).astype(BF16)
 
-    for tap in range(9):
-        spread(
-            parts_prior,
-            tap * chans,
-            scale * dot_in(x_ctx[1, pl.ds(w, cells), :], boxes[tap]),
-        )
-    prior_1()
-    prior_2()
     total = None
     for tap in range(9):
         part = dot_out(boxes[tap], tap_of(w_prior, tap // 3, tap % 3))
@@ -572,34 +637,45 @@
         (total[cells - w :],),
         (get(s_pool, pl.ds(stride + EDGE, h, stride=stride)),),
         (get(s_pool, pl.ds(stride + EDGE + w - 1, h, stride=stride)),),
-        (total[0:w],),
-        (total[0:w],),
-        (total[cells - w :],),
-        (total[cells - w :],),
     ]
-    found = start(2, (w, w), parts)
+    for k in range(4):
+        i, j = k // 2, k % 2
+        at = (i * (h - 1) + 1) * stride + EDGE + j * (w - 1)
+        parts.append(corner(k, get(s_pool, pl.ds(at, 1))))
+    found = start(2, (w, CORNER), parts)
+    for part in range(2):
+        for tap in range(9):
+            spread(
+                parts_prior[2 * part : 2 * part + 2],
+                tap * chans,
+                dot_in(
+                    x_ctx[1, pl.ds(w, cells), :], boxes[tap, :, part * chans : (part + 1) * chans]
+                ),
+            )
+        advance(prior_chains[2 * part : 2 * part + 2])
     gco = total.astype(BF16)
     for a in range(3):
         for b in range(3):
             spread(
                 parts_coarse,
                 (3 * a + b) * chans,
-                scale * dot_in(x_pool[b, pl.ds((a + 1) * w, cells), :], gco),
+                dot_in(x_pool[b, pl.ds((a + 1) * w, cells), :], gco),
             )
-    middle()
-    prior_1()
-    prior_2()
+    advance(early)
+    advance(middle_chains)
+    advance(late)
+    advance(middle_chains)
     finish(found)
 
     put(s_pool, pl.ds(EDGE, w), halo(2, UP, 0, w))
     put(s_pool, pl.ds((h + 1) * stride + EDGE, w), halo(2, DOWN, 0, w))
     put(s_pool, pl.ds(stride + EDGE - 1, h, stride=stride), halo(2, LEFT, 0, h))
     put(s_pool, pl.ds(stride + EDGE + w, h, stride=stride), halo(2, RIGHT, 0, h))
-    put(s_pool, pl.ds(EDGE - 1, 1), halo(2, UP_LEFT, 0, w)[w - 1 :])
-    put(s_pool, pl.ds(EDGE + w, 1), halo(2, UP_RIGHT, 0, w)[0:1])
+    put(s_pool, pl.ds(EDGE - 1, 1), halo(2, UP_LEFT, 0, CORNER)[0:1])
+    put(s_pool, pl.ds(EDGE + w, 1), halo(2, UP_RIGHT, 0, CORNER)[0:1])
     last = (h + 1) * stride + EDGE
-    put(s_pool, pl.ds(last - 1, 1), halo(2, DOWN_LEFT, 0, w)[w - 1 :])
-    put(s_pool, pl.ds(last + w, 1), halo(2, DOWN_RIGHT, 0, w)[0:1])
+    put(s_pool, pl.ds(last - 1, 1), halo(2, DOWN_LEFT, 0, CORNER)[0:1])
+    put(s_pool, pl.ds(last + w, 1), halo(2, DOWN_RIGHT, 0, CORNER)[0:1])
     for i in range(h + 2):
         for k in range(3):
             x_gco[k, i * w : (i + 1) * w, :] = get(
@@ -638,24 +714,23 @@
         (gfi_line(1, 0, h - 1), gfi_line(1, 1, h - 1)),
         (gfi_column(0, 0), gfi_column(1, 0)),
         (gfi_column(0, 1), gfi_column(1, 1)),
-        (gfi_line(0, 0, 0),),
-        (gfi_line(0, 1, 0),),
-        (gfi_line(1, 0, h - 1),),
-        (gfi_line(1, 1, h - 1),),
     ]
-    found = start(3, (2 * w, w), parts)
+    for k in range(4):
+        i, j = k // 2, k % 2
+        at = i * (2 * h - 1) * stride + EDGE + j * (w - 1)
+        parts.append(corner(k, get(s_gfi(j), pl.ds(at, 1))))
+    found = start(3, (2 * w, CORNER), parts)
     for a in range(3):
         for b in range(3):
             total = None
             for p, q in phases:
                 part = dot_in(view(x_feat, p + a - 1, q + b - 1), own_gfi[2 * p + q])
                 total = part if total is None else total + part
-            spread(parts_post, (3 * a + b) * chans, scale * total)
-    post_1()
-    post_2()
-    middle()
-    prior_1()
-    prior_2()
+            spread(parts_post, (3 * a + b) * chans, total)
+    advance(post_chains)
+    advance(post_chains)
+    advance(prior_chains)
+    advance(middle_chains)
     finish(found)
     for p in range(2):
         put(s_gfi(1), pl.ds(p * h * stride + EDGE - 1, h, stride=stride), halo(3, LEFT, p * h, h))
@@ -672,16 +747,14 @@
             x_gfi[p, 3, here, :] = get(s_gfi(0), pl.ds(at + 1, w)).astype(BF16)
         ring_at = slice((1 - p) * cells, (1 - p) * cells + w)
         vertical_side = UP if p else DOWN
-        left = halo(3, UP_LEFT if p else DOWN_LEFT, 0, w)[w - 1 :]
-        right = halo(3, UP_RIGHT if p else DOWN_RIGHT, 0, w)[0:1]
+        left = halo(3, UP_LEFT if p else DOWN_LEFT, 0, CORNER)[0:1]
+        right = halo(3, UP_RIGHT if p else DOWN_RIGHT, 0, CORNER)[0:1]
         put(s_gfi(1), pl.ds(EDGE - 1, 1), left)
         put(s_gfi(1), pl.ds(EDGE, w), halo(3, vertical_side, w, w))
         put(s_gfi(0), pl.ds(EDGE, w), halo(3, vertical_side, 0, w))
         put(s_gfi(0), pl.ds(EDGE + w, 1), right)
         x_gfi[p, 0, ring_at, :] = get(s_gfi(1), pl.ds(EDGE - 1, w)).astype(BF16)
         x_gfi[p, 3, ring_at, :] = get(s_gfi(0), pl.ds(EDGE + 1, w)).astype(BF16)
-    post_1()
-    post_2()
     for p, q in phases:
         total = None
         for a in range(3):
@@ -691,14 +764,36 @@
         for i in range(h):
             put(mix, pl.ds((2 * i + p) * cols + q, w, stride=2), total[i * w : (i + 1) * w])
     grad_feat[...] = get(mix, pl.ds(0, rows * cols)).astype(BF16)
-    for _ in range(bits + 1):
-        for step in (prior_1, prior_2, middle, post_1, post_2):
-            step()
+    stores[0].start()
+    advance(post_chains)
+    advance(prior_chains)
+    advance(middle_chains)
+    advance(post_chains)
+    advance(prior_chains)
+    advance(middle_chains)
+    for _ in range(bits):
+        advance(prior_chains + middle_chains + post_chains)
+    for store in stores[1:]:
+        store.start()
+    for store in stores:
+        store.wait()
 
 
 def hand_out(*refs):
     for source, target in zip(refs[:4], refs[4:]):
         target[...] = source[...]
+
+
+def orders_of(n_row, n_col, pieces):
+    bits = (n_row * n_col).bit_length() - 1
+    near, a, b = (0,), 1, n_col.bit_length() - 1
+    far = [k for k in range(1, bits) if k not in (a, b)]
+    pairs = [tuple(far[k : k + 2]) for k in range(0, len(far), 2)]
+    singles = [(k,) for k in far]
+    post = (near, (a, b), *pairs)
+    middle = (near, singles[0], (a, b), *singles[1:])
+    prior = ((near, (b,), (a,), *pairs), (near, (a,), (b,), *pairs))
+    return (post,) * pieces + (middle,) * pieces + prior * pieces
 
 
 def on_device(sizes, feat, noise_fine, noise_coarse, w_post, w_coarse, w_prior):
@@ -708,10 +803,12 @@
     scale = 1.0 / math.sqrt(rows * n_row * cols * n_col)
     cells, quarter = rows * cols, h * w
     vmem = pl.BlockSpec(memory_space=pltpu.VMEM)
-    dims = (rows, cols, chans, scale, n_row, n_col)
     count = n_row * n_col
+    orders = orders_of(n_row, n_col, chans // LANES)
+    dims = (rows, cols, chans, scale, n_row, n_col, orders)
     per = w_post.shape[0] // count
-    widths = (chans // 2, chans // 2, chans, chans, chans)
+    widths = (LANES,) * len(orders)
+    anywhere = pl.BlockSpec(memory_space=pl.ANY)
     extra, side, stride = round_up(h + 1, 16), round_up(h + 2, 8), w + 2 * EDGE
 
     def lanes(n, depth=chans):
@@ -725,9 +822,19 @@
             jax.ShapeDtypeStruct((per * chans // LANES, LANES), F32),
             jax.ShapeDtypeStruct((per * 2 * chans // LANES, LANES), F32),
         ),
-        in_specs=[vmem] * 6,
-        out_specs=(vmem,) * 4,
+        in_specs=[anywhere] * 6,
+        out_specs=(anywhere,) * 4,
         scratch_shapes=[
+            pltpu.VMEM((cells, chans), BF16),
+            pltpu.VMEM((cells, chans), F32),
+            pltpu.VMEM((quarter, chans), F32),
+            pltpu.VMEM(w_post.shape, BF16),
+            pltpu.VMEM(w_coarse.shape, BF16),
+            pltpu.VMEM(w_prior.shape, BF16),
+            pltpu.VMEM((cells, chans), BF16),
+            pltpu.VMEM((per * chans // LANES, LANES), F32),
+            pltpu.VMEM((per * chans // LANES, LANES), F32),
+            pltpu.VMEM((per * 2 * chans // LANES, LANES), F32),
             pltpu.VMEM((4, (h + 1) * w + extra, chans), F32),
             pltpu.VMEM((4, quarter, chans), F32),
             pltpu.VMEM((quarter, chans), F32),
@@ -736,6 +843,7 @@
             lanes(side * stride),
             lanes((extra + 1) * stride),
             pltpu.VMEM((2, 2 * chans // LANES, max(2 * h * stride, cells), LANES), F32),
+            lanes(4 * CORNER),
             pltpu.VMEM((2, 4, (h + 1) * w, chans), BF16),
             pltpu.VMEM((3, (h + 4) * w, chans), BF16),
             pltpu.VMEM((9, 2 * side, chans), BF16),
@@ -752,7 +860,9 @@
             [pltpu.VMEM((count // 2, per, width), BF16) for width in widths],
             [pltpu.VMEM((count - 1, per, width), BF16) for width in widths],
             pltpu.SemaphoreType.DMA((4, 16)),
-            pltpu.SemaphoreType.DMA((5, count.bit_length() - 1, 2)),
+            pltpu.SemaphoreType.DMA((len(orders), max(map(len, orders)), 3, 2)),
+            pltpu.SemaphoreType.DMA((6,)),
+            pltpu.SemaphoreType.DMA((4,)),
         ],
         compiler_params=pltpu.CompilerParams(
             collective_id=0, has_side_effects=True, vmem_limit_bytes=65000 * 1024

time: 59.4 us -> 55.5 us (0.934)
  Pallas kernels: 58.6 us -> 54.7 us
    pallas_call x1, Pallas kernels: 56.6 us -> 52.7 us  [on_device(): pl.pallas_call(functools.partial(tile_kernel, dims), out_shape=(jax.Shape...]
where the time goes in v2:
time: 55.5 us; the launch traced here: 55.4 us
  Pallas kernels  54.7 us (99%)
  between operations  0.64 us (1%)
    pallas_call x1, Pallas kernels, on_device(): pl.pallas_call(functools.partial(tile_kernel, dims), out_shape=(jax.Shape...  52.7 us
    pallas_call x1, Pallas kernels, on_device(): pl.pallas_call(hand_out, out_shape=tuple((jax.ShapeDtypeStruct(a.shape, a...  2.03 us

profile of v2, /device:TPU:0, one launch (start us, length us, event | category | flops | bytes accessed | tf_op | source)
XLA Modules:
  0.0 55.4 jit_solution(14669754949222858642)
XLA Ops:
  0.6 52.7 %shard_map.93 = (bf16[1024,256]{1,0:T(8,128)(2,1)}, f32[144,128]{1,0:T(8,128)}, f32[144,128]{1,0:T(8,128)}, f32[288,128]{1,0:T(8,128)}) custom-call(bf16[1024,256]{1,0:T(8,128)(2,1)} %bitcast.8, f32[1024,256]{1,0:T(8,128)} %bitcast.7, f32[256,256]{1,0:T(8,128)} %bitcast.9, bf16[2304,256]{1,0:T(8,128)(2,1)} %refs_3_.1, bf16[2304,256]{1,0:T(8,128)(2,1)} %refs_4_.1, ...), custom_call_target="tpu_custom_call" | custom-call | tf_op jit(solution)/shard_map/pallas_call | solution.py:817
  53.4 2.0 %shard_map.94 = (bf16[1024,256]{1,0:T(8,128)(2,1)}, f32[144,128]{1,0:T(8,128)}, f32[144,128]{1,0:T(8,128)}, f32[288,128]{1,0:T(8,128)}) custom-call(bf16[1024,256]{1,0:T(8,128)(2,1)} %get-tuple-element.12.refs_0_, f32[144,128]{1,0:T(8,128)} %get-tuple-element.13.refs_1_, f32[144,128]{1,0:T(8,128)} %get-tuple-element.14.refs_2_, ...), custom_call_target="tpu_custom_call" | custom-call | tf_op jit(solution)/shard_map/pallas_call | solution.py:879

commit v3 on v2

--- a/solution.py
+++ b/solution.py
@@ -40,7 +40,8 @@
     dims,
     *refs,
 ):
-    operands, results = refs[:6], refs[6:10]
+    operands = refs[:6]
+    grad_feat, out_post, out_coarse, out_prior = refs[6:10]
     (
         feat,
         noise_fine,
@@ -48,10 +49,6 @@
         w_post,
         w_coarse,
         w_prior,
-        grad_feat,
-        out_post,
-        out_coarse,
-        out_prior,
         fine,
         err,
         coarse,
@@ -79,15 +76,10 @@
         sems,
         chain_sems,
         load_sems,
-        store_sems,
     ) = refs[10:]
     loads = [
         pltpu.make_async_copy(source, target, load_sems.at[k])
         for k, (source, target) in enumerate(zip(operands, refs[10:16]))
-    ]
-    stores = [
-        pltpu.make_async_copy(source, target, store_sems.at[k])
-        for k, (source, target) in enumerate(zip(refs[16:20], results))
     ]
     for k in (0, 2, 5, 1, 3, 4):
         loads[k].start()
@@ -181,6 +173,27 @@
                 part = recv[bases[k] + (mask - 1) * lefts[k + 1] + slot].astype(F32)
                 total = part if total is None else total + part
             return total
+
+        def begin(half):
+            n = lefts[1] // 2
+            at = half * n
+            other = 1 - bit_of(order[0][0])
+
+            def fill(j):
+                send[at + j] = acc[2 * (at + j) + other].astype(BF16)
+
+            each(n, fill)
+            copy = pltpu.make_async_remote_copy(
+                src_ref=send.at[pl.ds(at, n)],
+                dst_ref=recv.at[pl.ds(at, n)],
+                send_sem=chain_sems.at[number, 0, half, 0],
+                recv_sem=chain_sems.at[number, 0, half, 1],
+                device_id=reach(order[0], 1),
+                device_id_type=pl.DeviceIdType.MESH,
+            )
+            copy.start()
+            state["copies"].append(copy)
+            state["step"] = 1
 
         def step():
             k = state["step"]
@@ -243,7 +256,7 @@
             if k > 0:
                 each(n, keep)
 
-        return step
+        return step, begin
 
 
     pieces = chans // LANES
@@ -257,8 +270,13 @@
     early, late = prior_chains[:2], prior_chains[2:]
 
     def advance(chains):
-        for step in chains:
+        for step, _begin in chains:
             step()
+
+    def begin(chains, tap):
+        if tap in (4, 8):
+            for _step, start_half in chains:
+                start_half(tap // 8)
 
     parts_post = [(sums[k], k * LANES) for k in range(pieces)]
     parts_coarse = [(sums[k + pieces], k * LANES) for k in range(pieces)]
@@ -586,8 +604,10 @@
         raw = prior[:, chans:]
         small = jnp.exp(-jnp.abs(raw))
         sigma = jnp.maximum(raw, 0.0) + jnp.log1p(small) + 0.5
-        gate = jnp.where(raw >= 0, 1.0, small) / (1.0 + small)
-        inverse = 1.0 / sigma
+        whole = 1.0 + small
+        both_inverse = 1.0 / (sigma * whole)
+        gate = jnp.where(raw >= 0, 1.0, small) * (sigma * both_inverse)
+        inverse = whole * both_inverse
         ratio = (fine[2 * p + q] - prior[:, :chans]) * inverse
         residual = ratio * inverse
         err[2 * p + q] = residual[own(p)]
@@ -652,7 +672,7 @@
                     x_ctx[1, pl.ds(w, cells), :], boxes[tap, :, part * chans : (part + 1) * chans]
                 ),
             )
-        advance(prior_chains[2 * part : 2 * part + 2])
+            begin(prior_chains[2 * part : 2 * part + 2], tap)
     gco = total.astype(BF16)
     for a in range(3):
         for b in range(3):
@@ -661,8 +681,8 @@
                 (3 * a + b) * chans,
                 dot_in(x_pool[b, pl.ds((a + 1) * w, cells), :], gco),
             )
+            begin(middle_chains, 3 * a + b)
     advance(early)
-    advance(middle_chains)
     advance(late)
     advance(middle_chains)
     finish(found)
@@ -727,7 +747,7 @@
                 part = dot_in(view(x_feat, p + a - 1, q + b - 1), own_gfi[2 * p + q])
                 total = part if total is None else total + part
             spread(parts_post, (3 * a + b) * chans, total)
-    advance(post_chains)
+            begin(post_chains, 3 * a + b)
     advance(post_chains)
     advance(prior_chains)
     advance(middle_chains)
@@ -764,7 +784,6 @@
         for i in range(h):
             put(mix, pl.ds((2 * i + p) * cols + q, w, stride=2), total[i * w : (i + 1) * w])
     grad_feat[...] = get(mix, pl.ds(0, rows * cols)).astype(BF16)
-    stores[0].start()
     advance(post_chains)
     advance(prior_chains)
     advance(middle_chains)
@@ -773,10 +792,6 @@
     advance(middle_chains)
     for _ in range(bits):
         advance(prior_chains + middle_chains + post_chains)
-    for store in stores[1:]:
-        store.start()
-    for store in stores:
-        store.wait()
 
 
 def hand_out(*refs):
@@ -817,13 +832,13 @@
     grad_feat, out_post, out_coarse, out_prior = pl.pallas_call(
         functools.partial(tile_kernel, dims),
         out_shape=(
-            jax.ShapeDtypeStruct((cells, chans), BF16),
-            jax.ShapeDtypeStruct((per * chans // LANES, LANES), F32),
-            jax.ShapeDtypeStruct((per * chans // LANES, LANES), F32),
-            jax.ShapeDtypeStruct((per * 2 * chans // LANES, LANES), F32),
+            pltpu.VMEM((cells, chans), BF16),
+            pltpu.VMEM((per * chans // LANES, LANES), F32),
+            pltpu.VMEM((per * chans // LANES, LANES), F32),
+            pltpu.VMEM((per * 2 * chans // LANES, LANES), F32),
         ),
         in_specs=[anywhere] * 6,
-        out_specs=(anywhere,) * 4,
+        out_specs=(vmem,) * 4,
         scratch_shapes=[
             pltpu.VMEM((cells, chans), BF16),
             pltpu.VMEM((cells, chans), F32),
@@ -831,10 +846,6 @@
             pltpu.VMEM(w_post.shape, BF16),
             pltpu.VMEM(w_coarse.shape, BF16),
             pltpu.VMEM(w_prior.shape, BF16),
-            pltpu.VMEM((cells, chans), BF16),
-            pltpu.VMEM((per * chans // LANES, LANES), F32),
-            pltpu.VMEM((per * chans // LANES, LANES), F32),
-            pltpu.VMEM((per * 2 * chans // LANES, LANES), F32),
             pltpu.VMEM((4, (h + 1) * w + extra, chans), F32),
             pltpu.VMEM((4, quarter, chans), F32),
             pltpu.VMEM((quarter, chans), F32),
@@ -862,10 +873,9 @@
             pltpu.SemaphoreType.DMA((4, 16)),
             pltpu.SemaphoreType.DMA((len(orders), max(map(len, orders)), 3, 2)),
             pltpu.SemaphoreType.DMA((6,)),
-            pltpu.SemaphoreType.DMA((4,)),
         ],
         compiler_params=pltpu.CompilerParams(
-            collective_id=0, has_side_effects=True, vmem_limit_bytes=65000 * 1024
+            collective_id=0, has_side_effects=True, vmem_limit_bytes=62 * 2**20
         ),
     )(
         feat.reshape(cells, chans),
@@ -875,7 +885,10 @@
         w_coarse,
         w_prior,
     )
-    results = (grad_feat, out_post, out_coarse, out_prior)
+    results = tuple(
+        pltpu.with_memory_space_constraint(a, pltpu.VMEM)
+        for a in (grad_feat, out_post, out_coarse, out_prior)
+    )
     grad_feat, out_post, out_coarse, out_prior = pl.pallas_call(
         hand_out,
         out_shape=tuple(jax.ShapeDtypeStruct(a.shape, a.dtype) for a in results),

time: 55.5 us -> 53.7 us (0.968)
  Pallas kernels: 54.7 us -> 52.9 us
    pallas_call x1, Pallas kernels: 2.03 us -> 0.94 us  [on_device(): pl.pallas_call(hand_out, out_shape=tuple((jax.ShapeDtypeStruct(a.shape, a...]
    pallas_call x1, Pallas kernels: 52.7 us -> 52 us  [on_device(): pl.pallas_call(functools.partial(tile_kernel, dims), out_shape=(pltpu.VME...]
where the time goes in v3:
time: 53.7 us; the launch traced here: 53.6 us
  Pallas kernels  52.9 us (99%)
  between operations  0.64 us (1%)
    pallas_call x1, Pallas kernels, on_device(): pl.pallas_call(functools.partial(tile_kernel, dims), out_shape=(pltpu.VME...  52 us

profile of v3, /device:TPU:0, one launch (start us, length us, event | category | flops | bytes accessed | tf_op | source)
XLA Modules:
  0.0 53.6 jit_solution(16112521769647256014)
XLA Ops:
  0.6 52.0 %shard_map.93 = (bf16[1024,256]{1,0:T(8,128)(2,1)S(1)}, f32[144,128]{1,0:T(8,128)S(1)}, f32[144,128]{1,0:T(8,128)S(1)}, f32[288,128]{1,0:T(8,128)S(1)}) custom-call(bf16[1024,256]{1,0:T(8,128)(2,1)} %bitcast.8, f32[1024,256]{1,0:T(8,128)} %bitcast.7, f32[256,256]{1,0:T(8,128)} %bitcast.9, bf16[2304,256]{1,0:T(8,128)(2,1)} %refs_3_.1, ...), custom_call_target="tpu_custom_call" | custom-call | tf_op jit(solution)/shard_map/pallas_call | solution.py:832
  52.6 0.9 %shard_map.94 = (bf16[1024,256]{1,0:T(8,128)(2,1)}, f32[144,128]{1,0:T(8,128)}, f32[144,128]{1,0:T(8,128)}, f32[288,128]{1,0:T(8,128)}) custom-call(bf16[1024,256]{1,0:T(8,128)(2,1)S(1)} %get-tuple-element.12.refs_0_, f32[144,128]{1,0:T(8,128)S(1)} %get-tuple-element.13.refs_1_, f32[144,128]{1,0:T(8,128)S(1)} %get-tuple-element.14.refs_2_, ...), custom_call_target="tpu_custom_call" | custom-call | tf_op jit(solution)/shard_map/pallas_call | solution.py:892

commit v4 on v3

--- a/solution.py
+++ b/solution.py
@@ -808,7 +808,8 @@
     post = (near, (a, b), *pairs)
     middle = (near, singles[0], (a, b), *singles[1:])
     prior = ((near, (b,), (a,), *pairs), (near, (a,), (b,), *pairs))
-    return (post,) * pieces + (middle,) * pieces + prior * pieces
+    mixed = ((post, middle)[k % 2] for k in range(pieces))
+    return (*mixed, *(middle,) * pieces, *prior * pieces)
 
 
 def on_device(sizes, feat, noise_fine, noise_coarse, w_post, w_coarse, w_prior):

time: 53.7 us -> 51.8 us (0.965)
  Pallas kernels: 52.9 us -> 51 us
    pallas_call x1, Pallas kernels: 52 us -> 50.1 us  [on_device(): pl.pallas_call(functools.partial(tile_kernel, dims), out_shape=(pltpu.VME...]
where the time goes in v4:
time: 51.8 us; the launch traced here: 51.7 us
  Pallas kernels  51 us (98%)
  between operations  0.64 us (1%)
    pallas_call x1, Pallas kernels, on_device(): pl.pallas_call(functools.partial(tile_kernel, dims), out_shape=(pltpu.VME...  50.1 us

profile of v4, /device:TPU:0, one launch (start us, length us, event | category | flops | bytes accessed | tf_op | source)
XLA Modules:
  0.0 51.7 jit_solution(11749924101689119928)
XLA Ops:
  0.6 50.1 %shard_map.93 = (bf16[1024,256]{1,0:T(8,128)(2,1)S(1)}, f32[144,128]{1,0:T(8,128)S(1)}, f32[144,128]{1,0:T(8,128)S(1)}, f32[288,128]{1,0:T(8,128)S(1)}) custom-call(bf16[1024,256]{1,0:T(8,128)(2,1)} %bitcast.8, f32[1024,256]{1,0:T(8,128)} %bitcast.7, f32[256,256]{1,0:T(8,128)} %bitcast.9, bf16[2304,256]{1,0:T(8,128)(2,1)} %refs_3_.1, ...), custom_call_target="tpu_custom_call" | custom-call | tf_op jit(solution)/shard_map/pallas_call | solution.py:833
  50.8 0.9 %shard_map.94 = (bf16[1024,256]{1,0:T(8,128)(2,1)}, f32[144,128]{1,0:T(8,128)}, f32[144,128]{1,0:T(8,128)}, f32[288,128]{1,0:T(8,128)}) custom-call(bf16[1024,256]{1,0:T(8,128)(2,1)S(1)} %get-tuple-element.12.refs_0_, f32[144,128]{1,0:T(8,128)S(1)} %get-tuple-element.13.refs_1_, f32[144,128]{1,0:T(8,128)S(1)} %get-tuple-element.14.refs_2_, ...), custom_call_target="tpu_custom_call" | custom-call | tf_op jit(solution)/shard_map/pallas_call | solution.py:893

commit v5 on v4

--- a/solution.py
+++ b/solution.py
@@ -314,7 +314,7 @@
 
     def start(index, sizes, parts):
         found = copies(index, sizes)
-        for d in (4, 5, 6, 7, 0, 1, 2, 3):
+        for d in (0, 1, 4, 5, 6, 7, 2, 3):
             at = 0
             for part in parts[d]:
                 edges[index, d, at : at + part.shape[0], :] = part.astype(BF16)

time: 51.8 us -> 52.2 us (level)
  no operation moved by 1% of the time
where the time goes in v5:
time: 52.2 us; the launch traced here: 52.1 us
  Pallas kernels  51.4 us (98%)
  between operations  0.64 us (1%)
    pallas_call x1, Pallas kernels, on_device(): pl.pallas_call(functools.partial(tile_kernel, dims), out_shape=(pltpu.VME...  50.5 us

profile of v5, /device:TPU:0, one launch (start us, length us, event | category | flops | bytes accessed | tf_op | source)
XLA Modules:
  0.0 52.1 jit_solution(1164467339947982616)
XLA Ops:
  0.6 50.5 %shard_map.93 = (bf16[1024,256]{1,0:T(8,128)(2,1)S(1)}, f32[144,128]{1,0:T(8,128)S(1)}, f32[144,128]{1,0:T(8,128)S(1)}, f32[288,128]{1,0:T(8,128)S(1)}) custom-call(bf16[1024,256]{1,0:T(8,128)(2,1)} %bitcast.8, f32[1024,256]{1,0:T(8,128)} %bitcast.7, f32[256,256]{1,0:T(8,128)} %bitcast.9, bf16[2304,256]{1,0:T(8,128)(2,1)} %refs_3_.1, ...), custom_call_target="tpu_custom_call" | custom-call | tf_op jit(solution)/shard_map/pallas_call | solution.py:833
  51.1 0.9 %shard_map.94 = (bf16[1024,256]{1,0:T(8,128)(2,1)}, f32[144,128]{1,0:T(8,128)}, f32[144,128]{1,0:T(8,128)}, f32[288,128]{1,0:T(8,128)}) custom-call(bf16[1024,256]{1,0:T(8,128)(2,1)S(1)} %get-tuple-element.12.refs_0_, f32[144,128]{1,0:T(8,128)S(1)} %get-tuple-element.13.refs_1_, f32[144,128]{1,0:T(8,128)S(1)} %get-tuple-element.14.refs_2_, ...), custom_call_target="tpu_custom_call" | custom-call | tf_op jit(solution)/shard_map/pallas_call | solution.py:893
